TPU v7x, 32 devices: a whole 2x2x4 slice. The times are simulated.
32 devices in a mesh: row: 8 (over z, x), col: 4 (over y, core).
Axes of the slice: x: 2, y: 2, z: 4, core: 2. Of those that a mesh axis runs over, the one named last changes fastest.
Arguments:
- x_vectors: bfloat16 [64, 32768], P(None, ('row', 'col')), may hold values from -6 to 6
- w_vectors: bfloat16 [64, 32768], P(None, ('row', 'col')), may hold values from -6 to 6
- order: int32 [32768], P(('row', 'col')), may hold values from 0 to 32767, as said below
- ubasis: bfloat16 [64, 32768], P(None, ('row', 'col')), may hold values from -0.75 to 0.75
- vbasis: bfloat16 [64, 32768], P(None, ('row', 'col')), may hold values from -0.75 to 0.75
- leaf_up_u: bfloat16 [64, 32768], P(None, ('row', 'col')), may hold values from -0.1875 to 0.1875
- leaf_up_v: bfloat16 [64, 32768], P(None, ('row', 'col')), may hold values from -0.1875 to 0.1875
- coupling: bfloat16 [64, 1048576], P(None, ('row', 'col')), may hold values from -0.1875 to 0.1875
- coupling_pairs: int32 [2, 16384], P(None, ('row', 'col')), may hold values from 0 to 511, as said below
- coupling_count: int32 [32], P(('row', 'col')), may hold values from 128 to 512, as said below
- near_blocks: bfloat16 [64, 524288], P(None, ('row', 'col')), may hold values from -0.1875 to 0.1875
- near_pairs: int32 [2, 8192], P(None, ('row', 'col')), may hold values from 0 to 511, as said below
- transfer_u: bfloat16 [64, 3840], replicated, may hold values from -0.5 to 0.5
- transfer_v: bfloat16 [64, 3840], replicated, may hold values from -0.5 to 0.5
- upper_coupling: bfloat16 [64, 3968], replicated, may hold values from -6 to 6
Outputs:
- y_product: bfloat16 [64, 32768], P(None, ('row', 'col'))
- z_product: bfloat16 [64, 32768], P(None, ('row', 'col'))
Inputs may be any that keep to these rules, and one draw needn't show every extreme that they name: `order`: each block of 1024 consecutive entries is a permutation of that block's own positions. `coupling_pairs`: for slot b let d = b // 512, r = d // 4, c = d % 4. Entry [0, b] is a leaf of row group r, that is from r * 4 * 16 to (r + 1) * 4 * 16 - 1; entry [1, b] is a leaf l with (l // 16) % 4 == c. Slots of block d from coupling_count[d] onward are not used. `near_pairs`: for slot n let d = n // 256, r = d // 4, c = d % 4. Entry [0, n] is a leaf of row group r as for coupling_pairs; entry [1, n] is a leaf l with t = l // 16, t % 4 == c and t // 4 equal to r - 1, r or r + 1 modulo 8.
All inputs are finite; a program needn't handle non-finite values.
Results may differ from a plain program's by a relative error of at most 0.0063.
Values may be sent and summed in bfloat16 or wider, within the bound.
A program may use at most 192 MiB of HBM per device.

v0:
```python
import functools

import jax
import jax.numpy as jnp
from jax import lax
from jax.experimental import pallas as pl
from jax.experimental.pallas import tpu as pltpu
from jax.sharding import PartitionSpec as P

BF = jnp.bfloat16
F32 = jnp.float32
VMEM = pl.BlockSpec(memory_space=pltpu.VMEM)
SMEM = pl.BlockSpec(memory_space=pltpu.SMEM)
NN = (((1,), (0,)), ((), ()))
NT = (((1,), (1,)), ((), ()))
VLIMIT = 60 * 1024 * 1024


def mm(a, b, dims=NN):
    return lax.dot_general(a, b, dims, preferred_element_type=F32)


def left_mask(half, dtype):
    lane = lax.broadcasted_iota(jnp.int32, (1, 2 * half), 1)
    return (lane < half).astype(F32).astype(dtype), (lane >= half).astype(F32).astype(dtype)


def diag2(v, ml, mr):
    return jnp.concatenate([v * ml, v * mr], axis=0)


def split2(v):
    hi = v.astype(BF)
    return hi, (v - hi.astype(F32)).astype(BF)


def mm2(v, b, dims):
    hi, lo = split2(v)
    return mm(hi, b, dims) + mm(lo, b, dims)


def one_hot(order_ref, base):
    n = order_ref.shape[1]
    src = lax.broadcasted_iota(jnp.int32, (n, n), 0)
    return jnp.where(src == order_ref[...] - base, 1.0, 0.0).astype(BF)


def up_kernel(base_ref, x_ref, w_ref, order_ref, v_ref, u_ref, ev_ref, eu_ref, xo_ref, wo_ref, xn_ref, wn_ref):
    q, n = x_ref.shape
    packs = xo_ref.shape[1]
    wide = xo_ref.shape[3]
    half = wide // 2
    ml, mr = left_mask(half, BF)
    hot = one_hot(order_ref, base_ref[0])
    both = mm(jnp.concatenate([x_ref[...], w_ref[...]], axis=0), hot).astype(BF)
    for side, (b_ref, e_ref, o_ref, n_ref) in enumerate(
        ((v_ref, ev_ref, xo_ref, xn_ref), (u_ref, eu_ref, wo_ref, wn_ref))
    ):
        pts = both[side * q:(side + 1) * q]
        node = jnp.zeros((q, wide), F32)
        for m in range(packs):
            cols = slice(m * wide, (m + 1) * wide)
            pm = pts[:, cols]
            cm = mm(pm, diag2(b_ref[:, cols], ml, mr), NT).astype(BF)
            o_ref[0, m] = cm
            o_ref[1, m] = pm
            node = node + mm(cm, diag2(e_ref[:, cols], ml, mr))
        n_ref[...] = (node + pltpu.roll(node, half, 1)).astype(BF)[:, :half]


def slot_kernel(ids_ref, x_ref, w_ref, s_ref, d_ref, y_ref, z_ref, xc, xp, wc, wp, yc, yn, zc, zn):
    rows, _, packs, q, wide = x_ref.shape
    cols = w_ref.shape[0]
    half = wide // 2
    ml, mr = left_mask(half, BF)
    slots = s_ref.shape[1] // half
    nears = d_ref.shape[1] // half
    o_row, o_col, n_row, n_col = 0, slots, 2 * slots, 2 * slots + nears
    live = ids_ref[2 * slots + 2 * nears]
    my_row = ids_ref[2 * slots + 2 * nears + 1]
    isl = lax.broadcasted_iota(jnp.int32, (q, wide), 1) < half
    lane = lax.broadcasted_iota(jnp.int32, (1, wide), 1)
    for acc in (yc, yn, zc, zn):
        def clear(i, carry, acc=acc):
            acc[i] = jnp.zeros(acc.shape[1:], F32)
            return carry
        lax.fori_loop(0, acc.shape[0], clear, 0)

    def widen(src, table, at):
        v = src[...].astype(F32)
        r = pltpu.roll(v, half, 1)
        table[at] = jnp.where(isl, v, r).astype(BF)
        table[at + 1] = jnp.where(isl, r, v).astype(BF)

    def fill_x(i, carry):
        for m in range(packs):
            widen(x_ref.at[i, 0, m], xc, 2 * (i * packs + m))
        return carry

    def fill_w(i, carry):
        for m in range(packs):
            widen(w_ref.at[i, 0, m], wc, 2 * (i * packs + m))
            widen(w_ref.at[i, 1, m], wp, 2 * (i * packs + m))
        return carry

    lax.fori_loop(0, rows, fill_x, 0)
    lax.fori_loop(0, cols, fill_w, 0)
    for k in range(3):
        src = lax.rem(my_row + (k + rows - 1), rows)
        for m in range(packs):
            widen(x_ref.at[src, 1, m], xp, 2 * (k * packs + m))

    def run(mat, xt, wt, ya, za, row_at, col_at, masked, steps, unroll):
        def step(g, carry):
            work = []
            for k in range(unroll):
                p = g * unroll + k
                i0, i1 = ids_ref[row_at + 2 * p], ids_ref[row_at + 2 * p + 1]
                j0, j1 = ids_ref[col_at + 2 * p], ids_ref[col_at + 2 * p + 1]
                blk = mat[:, pl.ds(pl.multiple_of(p * wide, wide), wide)]
                if masked:
                    left_ok = jnp.where(2 * p < live, 1.0, 0.0)
                    right_ok = jnp.where(2 * p + 1 < live, 1.0, 0.0)
                    a = jnp.where(lane < half, left_ok, 0.0).astype(BF)
                    b = jnp.where(lane < half, 0.0, right_ok).astype(BF)
                else:
                    a, b = ml, mr
                pair = jnp.concatenate([blk * a, blk * b], axis=0)
                xs = xt[j0] * ml + xt[j1] * mr
                ws = wt[i0] * ml + wt[i1] * mr
                work.append((i0, i1, j0, j1, mm(xs, pair, NT), mm(ws, pair)))
            for i0, i1, j0, j1, yv, zv in work:
                ya[i0] += jnp.where(isl, yv, 0.0)
                ya[i1] += jnp.where(isl, 0.0, yv)
                za[j0] += jnp.where(isl, zv, 0.0)
                za[j1] += jnp.where(isl, 0.0, zv)
            return carry
        lax.fori_loop(0, steps, step, 0)

    unroll = 4
    run(s_ref, xc, wc, yc, zc, o_row, o_col, True, (live + 2 * unroll - 1) // (2 * unroll), unroll)
    run(d_ref, xp, wp, yn, zn, n_row, n_col, False, nears // (2 * unroll), unroll)

    def fold(acc, at):
        a, b = acc[at], acc[at + 1]
        return jnp.where(isl, a + pltpu.roll(a, half, 1), b + pltpu.roll(b, half, 1))

    def out_y(i, carry):
        for m in range(packs):
            y_ref[i, 0, m] = fold(yc, 2 * (i * packs + m)).astype(y_ref.dtype)
            y_ref[i, 1, m] = fold(yn, 2 * (i * packs + m)).astype(y_ref.dtype)
        return carry

    def out_z(i, carry):
        rel = lax.rem(i - my_row + (rows + 1), rows)
        for m in range(packs):
            z_ref[i, 0, m] = fold(zc, 2 * (i * packs + m)).astype(z_ref.dtype)

        @pl.when(rel < 3)
        def _():
            for m in range(packs):
                z_ref[i, 1, m] = fold(zn, 2 * (rel * packs + m)).astype(z_ref.dtype)

        @pl.when(rel >= 3)
        def _():
            for m in range(packs):
                z_ref[i, 1, m] = jnp.zeros((q, wide), z_ref.dtype)
        return carry

    lax.fori_loop(0, cols, out_y, 0)
    lax.fori_loop(0, rows, out_z, 0)


def down_kernel(base_ref, y_ref, z_ref, yd_ref, zd_ref, order_ref, u_ref, v_ref, eu_ref, ev_ref, yo_ref, zo_ref):
    _, packs, q, wide = y_ref.shape
    half = wide // 2
    ml, mr = left_mask(half, BF)
    hot = one_hot(order_ref, base_ref[0])
    perms = []
    for s_ref, d_ref, b_ref, e_ref in ((y_ref, yd_ref, u_ref, eu_ref), (z_ref, zd_ref, v_ref, ev_ref)):
        down = jnp.concatenate([d_ref[...], d_ref[...]], axis=1)
        parts = []
        for m in range(packs):
            cs = slice(m * wide, (m + 1) * wide)
            leaf = (s_ref[0, m] + mm2(down, diag2(e_ref[:, cs], ml, mr), NT)).astype(BF)
            parts.append((mm(leaf, diag2(b_ref[:, cs], ml, mr)) + s_ref[1, m]).astype(BF))
        perms.append(jnp.concatenate(parts, axis=1))
    out = mm(jnp.concatenate(perms, axis=0), hot, NT).astype(BF)
    yo_ref[...] = out[:q]
    zo_ref[...] = out[q:]


def from_partner(block, axis, bit):
    count = lax.axis_size(axis)
    route = []
    for low in range(count):
        high = low | 1 << bit
        if high != low and high < count:
            route += [(low, high), (high, low)]
    return lax.ppermute(block, axis, route)


def node_block(matrix_set, node_id, node_width):
    return lax.dynamic_slice_in_dim(matrix_set, node_id * node_width, node_width, 1)


def tree(x_level, w_level, transfer_u, transfer_v, upper_coupling, rank):
    dev_count = lax.axis_size(("row", "col"))
    levels = dev_count.bit_length() - 1
    me = lax.axis_index(("row", "col"))
    y_terms, z_terms = [], []
    for level in range(levels):
        pair = jnp.concatenate([x_level, w_level], axis=1)
        sib = from_partner(pair, ("row", "col"), level)
        sib_x, sib_w = sib[:, :rank], sib[:, rank:]
        off = 2 * dev_count - 2 * (dev_count >> level)
        own = me >> level
        other = own ^ 1
        y_terms.append(mm(sib_x, node_block(upper_coupling, off + own, rank), NT))
        z_terms.append(mm(sib_w, node_block(upper_coupling, off + other, rank)))
        if level < levels - 1:
            x_level, w_level = (
                (mm(a, node_block(t, off + own, rank)) + mm(b, node_block(t, off + other, rank))).astype(BF)
                for a, b, t in ((x_level, sib_x, transfer_v), (w_level, sib_w, transfer_u))
            )
    y_down, z_down = y_terms[-1], z_terms[-1]
    for level in range(levels - 2, -1, -1):
        off = 2 * dev_count - 2 * (dev_count >> level)
        own = me >> level
        y_down = y_terms[level] + mm2(y_down, node_block(transfer_u, off + own, rank), NT)
        z_down = z_terms[level] + mm2(z_down, node_block(transfer_v, off + own, rank), NT)
    return y_down, z_down


def per_device(
    x_vectors,
    w_vectors,
    order,
    ubasis,
    vbasis,
    leaf_up_u,
    leaf_up_v,
    coupling,
    coupling_pairs,
    coupling_count,
    near_blocks,
    near_pairs,
    transfer_u,
    transfer_v,
    upper_coupling,
):
    q, piece = x_vectors.shape
    rank = ubasis.shape[0]
    leaves = leaf_up_u.shape[1] // rank
    packs = leaves // 2
    wide = 2 * rank
    slots = coupling_pairs.shape[1]
    nears = near_pairs.shape[1]
    rows = lax.axis_size("row")
    cols = lax.axis_size("col")
    me = lax.axis_index(("row", "col"))
    my_row = lax.axis_index("row")
    base = (me * piece).astype(jnp.int32).reshape(1)
    row_base = my_row * cols * leaves
    order2 = order.reshape(1, piece)
    params = pltpu.CompilerParams(vmem_limit_bytes=VLIMIT)
    x_out, w_out, x_node, w_node = pl.pallas_call(
        up_kernel,
        out_shape=(
            jax.ShapeDtypeStruct((2, packs, q, wide), BF),
            jax.ShapeDtypeStruct((2, packs, q, wide), BF),
            jax.ShapeDtypeStruct((q, rank), BF),
            jax.ShapeDtypeStruct((q, rank), BF),
        ),
        in_specs=[SMEM] + [VMEM] * 7,
        out_specs=(VMEM,) * 4,
        compiler_params=params,
    )(base, x_vectors, w_vectors, order2, vbasis, ubasis, leaf_up_v, leaf_up_u)
    x_all = lax.all_gather(x_out, "row", axis=0)
    w_all = lax.all_gather(w_out, "col", axis=0)
    tiles = near_pairs[1] // leaves // cols
    ids = jnp.concatenate(
        [
            coupling_pairs[0] - row_base,
            coupling_pairs[1] // leaves // cols * leaves + coupling_pairs[1] % leaves,
            near_pairs[0] - row_base,
            (tiles - my_row + rows + 1) % rows * leaves + near_pairs[1] % leaves,
            coupling_count,
            my_row.reshape(1).astype(jnp.int32),
        ]
    )
    y_part, z_part = pl.pallas_call(
        slot_kernel,
        out_shape=(
            jax.ShapeDtypeStruct((cols, 2, packs, q, wide), F32),
            jax.ShapeDtypeStruct((rows, 2, packs, q, wide), F32),
        ),
        in_specs=[SMEM] + [VMEM] * 4,
        out_specs=(VMEM,) * 2,
        scratch_shapes=[
            pltpu.VMEM((rows * leaves, q, wide), BF),
            pltpu.VMEM((3 * leaves, q, wide), BF),
            pltpu.VMEM((cols * leaves, q, wide), BF),
            pltpu.VMEM((cols * leaves, q, wide), BF),
            pltpu.VMEM((cols * leaves, q, wide), F32),
            pltpu.VMEM((cols * leaves, q, wide), F32),
            pltpu.VMEM((rows * leaves, q, wide), F32),
            pltpu.VMEM((3 * leaves, q, wide), F32),
        ],
        compiler_params=params,
    )(ids, x_all, w_all, coupling, near_blocks)
    y_down, z_down = tree(x_node, w_node, transfer_u, transfer_v, upper_coupling, rank)
    y_own = lax.psum_scatter(y_part, "col", scatter_dimension=0, tiled=False)
    z_own = lax.psum_scatter(z_part, "row", scatter_dimension=0, tiled=False)
    return pl.pallas_call(
        down_kernel,
        out_shape=(jax.ShapeDtypeStruct((q, piece), BF),) * 2,
        in_specs=[SMEM] + [VMEM] * 9,
        out_specs=(VMEM,) * 2,
        compiler_params=params,
    )(base, y_own, z_own, y_down, z_down, order2, ubasis, vbasis, leaf_up_u, leaf_up_v)


def solution(mesh):
    both = P(None, ("row", "col"))
    flat = P(("row", "col"))
    return jax.shard_map(
        per_device,
        mesh=mesh,
        in_specs=(both, both, flat, both, both, both, both, both, both, flat, both, both, P(), P(), P()),
        out_specs=(both, both),
        check_vma=False,
    )
```

profile of v0, /device:TPU:0, one launch (start us, length us, event | category | flops | bytes accessed | tf_op | source)
XLA Modules:
  0.0 252.0 jit_solution(8899902186361850117)
XLA Ops:
  7.2 3.2 %shard_map.158 = (bf16[2,8,64,128]{3,2,1,0:T(8,128)(2,1)}, bf16[2,8,64,128]{3,2,1,0:T(8,128)(2,1)}, bf16[64,64]{1,0:T(8,128)(2,1)}, bf16[64,64]{1,0:T(8,128)(2,1)}) custom-call(s32[1]{0:T(128)} %bitcast.base_ref, bf16[64,1024]{1,0:T(8,128)(2,1)} %x_ref.1, bf16[64,1024]{1,0:T(8,128)(2,1)} %w_ref.1, s32[1,1024]{1,0:T(1,128)} %bitcast.23, ...), custom_call_target="tpu_custom_call" | custom-call | tf_op jit(solution)/shard_map/pallas_call | solution.py:267
  10.5 0.7 all-gather.5.cloned.1.call-update
  11.9 0.8 fusion.153
  12.7 0.8 fusion.152
  13.5 0.7 concatenate.18.ids_ref
  14.1 15.9 %all-gather.7.cloned.1.call-done = bf16[8,8,64,128]{3,2,1,0:T(8,128)(2,1)} async-done(((bf16[2,8,64,128]{3,2,1,0:T(8,128)(2,1)}), bf16[8,8,64,128]{3,2,1,0:T(8,128)(2,1)}) %all-gather.7.cloned.1.call-update) | async-done | bytes 1048592 | tf_op jit(solution)/shard_map/all_gather | solution.py:280
  30.0 51.2 %all-gather.5.cloned.1.call-done = bf16[16,8,64,128]{3,2,1,0:T(8,128)(2,1)} async-done(((bf16[2,8,64,128]{3,2,1,0:T(8,128)(2,1)}), bf16[16,8,64,128]{3,2,1,0:T(8,128)(2,1)}) %all-gather.5.cloned.1.call-update) | async-done | bytes 2097168 | tf_op jit(solution)/shard_map/all_gather | solution.py:279
  81.3 28.8 %shard_map.159 = (f32[4,2,8,64,128]{4,3,2,1,0:T(8,128)}, f32[8,2,8,64,128]{4,3,2,1,0:T(8,128)}) custom-call(s32[1538]{0:T(1024)} %concatenate.18.ids_ref, bf16[8,2,8,64,128]{4,3,2,1,0:T(8,128)(2,1)} %bitcast.19, bf16[4,2,8,64,128]{4,3,2,1,0:T(8,128)(2,1)} %bitcast.20, bf16[64,32768]{1,0:T(8,128)(2,1)} %s_ref.1, bf16[64,16384]{1,0:T(8,128)(2,1)} %d_ref.1), custom_call_target="tpu_custom_call" | custom-call | tf_op jit(solution)/shard_map/pallas_call | solution.py:292
  110.2 0.6 copy-done.3
  110.9 0.2 copy-done.1
  111.1 0.2 fusion.79
  111.3 0.2 fusion.84
  111.5 0.5 collective-permute-done
  112.1 0.2 fusion.1
  112.3 0.2 fusion
  112.6 1.5 collective-permute-start.1
  114.0 0.2 fusion.69
  114.2 0.2 fusion.74
  114.5 1.8 collective-permute-done.1
  116.3 0.2 fusion.3
  116.5 0.2 fusion.2
  116.8 0.2 fusion.59
  117.0 0.2 fusion.64
  117.2 3.3 %collective-permute-done.2 = bf16[64,128]{1,0:T(8,128)(2,1)S(1)} collective-permute-done((bf16[64,128]{1,0:T(8,128)(2,1)S(1)}, bf16[64,128]{1,0:T(8,128)(2,1)S(1)}, u32[]{:S(2)}, u32[]{:S(2)}) %collective-permute-start.2) | collective-permute-done | bytes 16416 | tf_op jit(solution)/shard_map/ppermute | solution.py:200
  120.5 0.2 fusion.5
  120.7 0.2 fusion.4
  120.9 0.1 pad_maximum_fusion.3
  121.0 8.8 %collective-permute-start.3 = (bf16[64,128]{1,0:T(8,128)(2,1)S(1)}, bf16[64,128]{1,0:T(8,128)(2,1)S(1)}, u32[]{:S(2)}, u32[]{:S(2)}) collective-permute-start(bf16[64,128]{1,0:T(8,128)(2,1)S(1)} %pad_maximum_fusion.3), channel_id=1, source_target_pairs={{0,8},{8,0},{1,9},{9,1},{2,10},{10,2},{3,11},{11,3},{4,12},{12,4},... | collective-permute-start | bytes 49160 | tf_op jit(solution)/shard_map/ppermute | solution.py:200
  129.8 0.2 fusion.49
  130.0 0.2 fusion.54
  130.2 1.3 collective-permute-done.3
  131.5 0.2 fusion.7
  131.7 0.2 fusion.6
  132.0 1.7 collective-permute-start.4
  133.7 3.0 %collective-permute-done.4 = bf16[64,128]{1,0:T(8,128)(2,1)S(1)} collective-permute-done((bf16[64,128]{1,0:T(8,128)(2,1)S(1)}, bf16[64,128]{1,0:T(8,128)(2,1)S(1)}, u32[]{:S(2)}, u32[]{:S(2)}) %collective-permute-start.4) | collective-permute-done | bytes 16416 | tf_op jit(solution)/shard_map/ppermute | solution.py:200
  136.6 0.2 fusion.10
  136.8 0.2 fusion.8
  137.1 0.2 fusion.47
  137.2 0.2 convolution_add_fusion.11
  137.5 0.2 convolution_add_fusion.14
  137.7 0.2 fusion.57
  137.9 0.2 convolution_add_fusion.10
  138.1 0.2 convolution_add_fusion.17
  138.3 0.2 fusion.67
  138.5 0.2 convolution_add_fusion.9
  138.7 0.2 convolution_add_fusion.20
  138.9 0.2 fusion.77
  139.2 0.2 fusion.52
  139.4 0.2 convolution_add_fusion.3
  139.6 0.2 convolution_add_fusion.4
  139.8 0.2 fusion.62
  140.0 0.2 convolution_add_fusion.2
  140.2 0.2 convolution_add_fusion.5
  140.4 0.2 fusion.72
  140.6 0.2 convolution_add_fusion.1
  140.8 0.2 convolution_add_fusion.6
  141.1 0.2 fusion.82
  141.2 0.2 convolution_add_fusion.8
  141.5 0.8 convolution_add_fusion.23.yd_ref
  142.3 0.2 convolution_add_fusion
  142.5 0.8 convolution_add_fusion.7.zd_ref
  143.3 4.5 %reduce-scatter.3.cloned.1.call-done = f32[1,2,8,64,128]{4,3,2,1,0:T(8,128)} async-done(((f32[4,2,8,64,128]{4,3,2,1,0:T(8,128)}), f32[1,2,8,64,128]{4,3,2,1,0:T(8,128)}) %reduce-scatter.3.cloned.1.call-update) | async-done | bytes 524304 | tf_op jit(solution)/shard_map/reduce_scatter | solution.py:313
  147.8 91.9 %reduce-scatter.5.cloned.1.call-done = f32[1,2,8,64,128]{4,3,2,1,0:T(8,128)} async-done(((f32[8,2,8,64,128]{4,3,2,1,0:T(8,128)}), f32[1,2,8,64,128]{4,3,2,1,0:T(8,128)}) %reduce-scatter.5.cloned.1.call-update) | async-done | bytes 524304 | tf_op jit(solution)/shard_map/reduce_scatter | solution.py:314
  239.7 5.8 %shard_map.160 = (bf16[64,1024]{1,0:T(8,128)(2,1)}, bf16[64,1024]{1,0:T(8,128)(2,1)}) custom-call(s32[1]{0:T(128)} %bitcast.base_ref, f32[2,8,64,128]{3,2,1,0:T(8,128)} %bitcast.21, f32[2,8,64,128]{3,2,1,0:T(8,128)} %bitcast.22, f32[64,64]{1,0:T(8,128)} %convolution_add_fusion.23.yd_ref, f32[64,64]{1,0:T(8,128)} %convolution_add_fusion.7.zd_ref, ...), custom_call_target="tpu_custom_call" | custom-call | tf_op jit(solution)/shard_map/pallas_call | solution.py:315
  (23 shorter events, 0.7 us)
Async XLA Ops:
  7.2 129.5 %copy-start = (bf16[64,3968]{1,0:T(8,128)(2,1)S(1)}, bf16[64,3968]{1,0:T(8,128)(2,1)}, u32[]{:S(2)}) copy-start(bf16[64,3968]{1,0:T(8,128)(2,1)} %param.29) | copy-start | bytes 1523716
  7.2 22.8 %all-gather.7.cloned.1.call-start = ((), (), s32[]{:S(2)}) async-start(), calls=%async_computation.5 | async-start | bytes 1310720 | tf_op jit(solution)/shard_map/all_gather | solution.py:280
  10.4 70.8 %all-gather.5.cloned.1.call-start = ((), (), s32[]{:S(2)}) async-start(), calls=%async_computation.4 | async-start | bytes 2359296 | tf_op jit(solution)/shard_map/all_gather | solution.py:279
  11.2 136.6 %reduce-scatter.3.cloned.1.call-start = ((), (), s32[]{:S(2)}) async-start(), calls=%async_computation.2 | async-start | bytes 2621440 | tf_op jit(solution)/shard_map/reduce_scatter | solution.py:313
  110.1 0.7 copy-start.3
  110.1 0.7 copy-start.4
  110.1 1.1 copy-start.1
  110.1 1.3 copy-start.2
  110.1 129.6 %reduce-scatter.5.cloned.1.call-start = ((), (), s32[]{:S(2)}) async-start(), calls=%async_computation.3 | async-start | bytes 4718592 | tf_op jit(solution)/shard_map/reduce_scatter | solution.py:314
  110.9 1.2 collective-permute-start
  112.6 3.7 %collective-permute-start.1 = (bf16[64,128]{1,0:T(8,128)(2,1)S(1)}, bf16[64,128]{1,0:T(8,128)(2,1)S(1)}, u32[]{:S(2)}, u32[]{:S(2)}) collective-permute-start(bf16[64,128]{1,0:T(8,128)(2,1)S(1)} %pad_maximum_fusion.1), channel_id=1, source_target_pairs={{0,2},{2,0},{1,3},{3,1},{4,6},{6,4},{5,7},{7,5},{8,10},{10,8},{9,1... | collective-permute-start | bytes 49160 | tf_op jit(solution)/shard_map/ppermute | solution.py:200
  116.8 3.7 %collective-permute-start.2 = (bf16[64,128]{1,0:T(8,128)(2,1)S(1)}, bf16[64,128]{1,0:T(8,128)(2,1)S(1)}, u32[]{:S(2)}, u32[]{:S(2)}) collective-permute-start(bf16[64,128]{1,0:T(8,128)(2,1)S(1)} %pad_maximum_fusion.2), channel_id=1, source_target_pairs={{0,4},{4,0},{1,5},{5,1},{2,6},{6,2},{3,7},{7,3},{8,12},{12,8},{9,1... | collective-permute-start | bytes 49160 | tf_op jit(solution)/shard_map/ppermute | solution.py:200
  121.0 10.5 %collective-permute-start.3 = (bf16[64,128]{1,0:T(8,128)(2,1)S(1)}, bf16[64,128]{1,0:T(8,128)(2,1)S(1)}, u32[]{:S(2)}, u32[]{:S(2)}) collective-permute-start(bf16[64,128]{1,0:T(8,128)(2,1)S(1)} %pad_maximum_fusion.3), channel_id=1, source_target_pairs={{0,8},{8,0},{1,9},{9,1},{2,10},{10,2},{3,11},{11,3},{4,12},{12,4},... | collective-permute-start | bytes 49160 | tf_op jit(solution)/shard_map/ppermute | solution.py:200
  132.0 4.6 %collective-permute-start.4 = (bf16[64,128]{1,0:T(8,128)(2,1)S(1)}, bf16[64,128]{1,0:T(8,128)(2,1)S(1)}, u32[]{:S(2)}, u32[]{:S(2)}) collective-permute-start(bf16[64,128]{1,0:T(8,128)(2,1)S(1)} %pad_maximum_fusion.4), channel_id=1, source_target_pairs={{0,16},{16,0},{1,17},{17,1},{2,18},{18,2},{3,19},{19,3},{4,20},{20... | collective-permute-start | bytes 49160 | tf_op jit(solution)/shard_map/ppermute | solution.py:200
Sparse Core Ops, SparseCore 0:
  10.6 19.4 all-gather.6
  32.1 49.0 all-gather.4
  110.2 37.5 reduce-scatter.2
  151.3 88.3 reduce-scatter.4
where the time goes:
time: 252 us
  waiting for transfers between devices  174 us (69%)
  Pallas kernels  37.8 us (15%)
  between operations  14.5 us (6%)
  starting transfers between devices  12.1 us (5%)
  matrix products  9.84 us (4%)
    reduce_scatter x1, waiting for transfers between devices, per_device(): z_own = lax.psum_scatter(z_part, 'row', scatter_dimension=0, tiled=False)  91.9 us
    all_gather x1, waiting for transfers between devices, per_device(): x_all = lax.all_gather(x_out, 'row', axis=0)  51.2 us
    pallas_call x1, Pallas kernels, per_device(): pl.pallas_call(slot_kernel, out_shape=(jax.ShapeDtypeStruct((cols, 2, pac...  28.8 us
    all_gather x1, waiting for transfers between devices, per_device(): w_all = lax.all_gather(w_out, 'col', axis=0)  15.9 us
    ppermute x5, starting transfers between devices, from_partner(): return lax.ppermute(block, axis, route)  11.9 us
    ppermute x5, waiting for transfers between devices, from_partner(): return lax.ppermute(block, axis, route)  10 us
    dot_general x42, matrix products, mm(): return lax.dot_general(a, b, dims, preferred_element_type=F32)  9.84 us
    pallas_call x1, Pallas kernels, per_device(): pl.pallas_call(down_kernel, out_shape=(jax.ShapeDtypeStruct((q, piece), B...  5.78 us
  transfers between devices with their start and end apart: 9, of which 9 were waited for; matrix products, arithmetic and copies ran while one was open for 5% of the time, Pallas kernels for 0%

commit v1 on v0

v1 whole, which is shorter than its diff:
```python
import functools

import jax
import jax.numpy as jnp
from jax import lax
from jax.experimental import pallas as pl
from jax.experimental.pallas import tpu as pltpu
from jax.sharding import PartitionSpec as P

BF = jnp.bfloat16
F32 = jnp.float32
VMEM = pl.BlockSpec(memory_space=pltpu.VMEM)
SMEM = pl.BlockSpec(memory_space=pltpu.SMEM)
NN = (((1,), (0,)), ((), ()))
NT = (((1,), (1,)), ((), ()))
VLIMIT = 60 * 1024 * 1024


def mm(a, b, dims=NN):
    return lax.dot_general(a, b, dims, preferred_element_type=F32)


def left_mask(half, dtype):
    lane = lax.broadcasted_iota(jnp.int32, (1, 2 * half), 1)
    return (lane < half).astype(F32).astype(dtype), (lane >= half).astype(F32).astype(dtype)


def diag2(v, ml, mr):
    return jnp.concatenate([v * ml, v * mr], axis=0)


def split2(v):
    hi = v.astype(BF)
    return hi, (v - hi.astype(F32)).astype(BF)


def mm2(v, b, dims):
    hi, lo = split2(v)
    return mm(hi, b, dims) + mm(lo, b, dims)


def one_hot(order_ref, base):
    n = order_ref.shape[1]
    src = lax.broadcasted_iota(jnp.int32, (n, n), 0)
    return jnp.where(src == order_ref[...] - base, 1.0, 0.0).astype(BF)


def grid_of(rows):
    inner = 1 << ((rows.bit_length() - 1) // 2)
    return rows // inner, inner


def greet(rows, cols, r, c):
    bar = pltpu.get_barrier_semaphore()
    for d in range(1, rows):
        pl.semaphore_signal(bar, inc=1, device_id={"row": lax.rem(r + d, rows)}, device_id_type=pl.DeviceIdType.MESH)
    for d in range(1, cols):
        pl.semaphore_signal(bar, inc=1, device_id={"col": lax.rem(c + d, cols)}, device_id_type=pl.DeviceIdType.MESH)
    return bar


def push(src, dst, sems, at, axis, peer):
    copy = pltpu.make_async_remote_copy(
        src_ref=src,
        dst_ref=dst,
        send_sem=sems.at[(0, *at)],
        recv_sem=sems.at[(1, *at)],
        device_id={axis: peer},
        device_id_type=pl.DeviceIdType.MESH,
    )
    copy.start()
    return copy


def chunk_at(ref, at, wide):
    return ref[:, pl.ds(pl.multiple_of(at * wide, wide), wide)]


def combine(v0, v1, fv, fu, ml, mr, isl, half):
    xp = jnp.where(isl, v0, pltpu.roll(v1, half, 1)).astype(BF)
    wp = jnp.where(isl, pltpu.roll(v0, half, 1), v1).astype(BF)
    x = mm(xp, diag2(fv, ml, mr))
    w = mm(wp, diag2(fu, ml, mr))
    return jnp.where(isl, x + pltpu.roll(x, half, 1), w + pltpu.roll(w, half, 1)).astype(BF)


def up_kernel(rows, cols, x_ref, w_ref, order_ref, v_ref, u_ref, ev_ref, eu_ref, fu_ref, fv_ref,
              xc_ref, xp_ref, wa_ref, n0_ref, n2_ref, na_sem, nb_sem, z_sem, x_sem, p_sem, w_sem):
    q, n = x_ref.shape
    packs = xc_ref.shape[1]
    wide = xc_ref.shape[3]
    half = wide // 2
    deep, inner = grid_of(rows)
    r = lax.axis_index("row")
    c = lax.axis_index("col")
    zi = r // inner
    xi = lax.rem(r, inner)
    bar = greet(rows, cols, r, c)
    ml, mr = left_mask(half, BF)
    isl = lax.broadcasted_iota(jnp.int32, (q, wide), 1) < half
    hot = one_hot(order_ref, (r * cols + c) * n)
    both = mm(jnp.concatenate([x_ref[...], w_ref[...]], axis=0), hot).astype(BF)
    folds = []
    for side, (b_ref, e_ref) in enumerate(((v_ref, ev_ref), (u_ref, eu_ref))):
        pts = both[side * q:(side + 1) * q]
        node = jnp.zeros((q, wide), F32)
        for m in range(packs):
            cs = slice(m * wide, (m + 1) * wide)
            pm = pts[:, cs]
            cm = mm(pm, diag2(b_ref[:, cs], ml, mr), NT).astype(BF)
            if side == 0:
                xc_ref[r, m] = cm
                xp_ref[1, m] = pm
            else:
                wa_ref[c, 0, m] = cm
                wa_ref[c, 1, m] = pm
            node = node + mm(cm, diag2(e_ref[:, cs], ml, mr))
        folds.append(node + pltpu.roll(node, half, 1))
    n0_ref[c] = jnp.where(isl, folds[0], folds[1]).astype(BF)
    pl.semaphore_wait(bar, rows + cols - 2)
    node_a = [
        push(n0_ref.at[c], n0_ref.at[c], na_sem, (d - 1,), "col", lax.rem(c + d, cols)) for d in range(1, cols)
    ]
    own = xc_ref.at[r]
    along = [
        push(own, own, z_sem, (d - 1,), "row", lax.rem(zi + d, deep) * inner + xi) for d in range(1, deep)
    ]
    across = [
        push(own, own, x_sem, (0, d - 1), "row", zi * inner + lax.rem(xi + d, inner)) for d in range(1, inner)
    ]
    points = [
        push(xp_ref.at[1], xp_ref.at[0], p_sem, (0,), "row", lax.rem(r + 1, rows)),
        push(xp_ref.at[1], xp_ref.at[2], p_sem, (1,), "row", lax.rem(r + rows - 1, rows)),
    ]
    wide_w = [
        push(wa_ref.at[c], wa_ref.at[c], w_sem, (d - 1,), "col", lax.rem(c + d, cols)) for d in range(1, cols)
    ]
    for copy in node_a:
        copy.wait_recv()
    dev_count = rows * cols
    vals = [n0_ref[i].astype(F32) for i in range(cols)]
    level = 0
    while len(vals) > 1:
        off = dev_count - (dev_count >> level)
        count = len(vals) // 2
        nxt = []
        for i in range(count):
            at = off + r * count + i
            nxt.append(
                combine(vals[2 * i], vals[2 * i + 1], chunk_at(fv_ref, at, wide), chunk_at(fu_ref, at, wide), ml, mr, isl, half)
            )
        vals = [v.astype(F32) for v in nxt]
        level += 1
    n2_ref[r] = vals[0].astype(BF)
    node_b = [
        push(n2_ref.at[r], n2_ref.at[r], nb_sem, (d - 1,), "row", lax.rem(r + d, rows)) for d in range(1, rows)
    ]
    for d in range(1, deep):
        along[d - 1].wait_recv()
        got = xc_ref.at[lax.rem(zi + deep - d, deep) * inner + xi]
        across += [
            push(got, got, x_sem, (d, e - 1), "row", zi * inner + lax.rem(xi + e, inner)) for e in range(1, inner)
        ]
    for copy in node_b + across + points + wide_w:
        copy.wait_recv()
    for copy in node_a + node_b + along + across + points + wide_w:
        copy.wait_send()


def slot_kernel(ids_ref, x_ref, p_ref, w_ref, s_ref, d_ref, y_ref, z_ref, n_ref, xc, xp, wc, wp, yc, yn, zc, zn):
    rows, packs, q, wide = x_ref.shape
    cols = w_ref.shape[0]
    half = wide // 2
    ml, mr = left_mask(half, BF)
    slots = s_ref.shape[1] // half
    nears = d_ref.shape[1] // half
    o_row, o_col, n_row, n_col = 0, slots, 2 * slots, 2 * slots + nears
    live = ids_ref[2 * slots + 2 * nears]
    isl = lax.broadcasted_iota(jnp.int32, (q, wide), 1) < half
    lane = lax.broadcasted_iota(jnp.int32, (1, wide), 1)
    for acc in (yc, yn, zc, zn):
        def clear(i, carry, acc=acc):
            acc[i] = jnp.zeros(acc.shape[1:], F32)
            return carry
        lax.fori_loop(0, acc.shape[0], clear, 0)

    def widen(src, table, at):
        v = src[...].astype(F32)
        r = pltpu.roll(v, half, 1)
        table[at] = jnp.where(isl, v, r).astype(BF)
        table[at + 1] = jnp.where(isl, r, v).astype(BF)

    def fill_x(i, carry):
        for m in range(packs):
            widen(x_ref.at[i, m], xc, 2 * (i * packs + m))
        return carry

    def fill_w(i, carry):
        for m in range(packs):
            widen(w_ref.at[i, 0, m], wc, 2 * (i * packs + m))
            widen(w_ref.at[i, 1, m], wp, 2 * (i * packs + m))
        return carry

    lax.fori_loop(0, rows, fill_x, 0)
    lax.fori_loop(0, cols, fill_w, 0)
    for k in range(3):
        for m in range(packs):
            widen(p_ref.at[k, m], xp, 2 * (k * packs + m))

    def run(mat, xt, wt, ya, za, row_at, col_at, masked, steps, unroll):
        def step(g, carry):
            work = []
            for k in range(unroll):
                p = g * unroll + k
                i0, i1 = ids_ref[row_at + 2 * p], ids_ref[row_at + 2 * p + 1]
                j0, j1 = ids_ref[col_at + 2 * p], ids_ref[col_at + 2 * p + 1]
                blk = mat[:, pl.ds(pl.multiple_of(p * wide, wide), wide)]
                if masked:
                    left_ok = jnp.where(2 * p < live, 1.0, 0.0)
                    right_ok = jnp.where(2 * p + 1 < live, 1.0, 0.0)
                    a = jnp.where(lane < half, left_ok, 0.0).astype(BF)
                    b = jnp.where(lane < half, 0.0, right_ok).astype(BF)
                else:
                    a, b = ml, mr
                pair = jnp.concatenate([blk * a, blk * b], axis=0)
                xs = xt[j0] * ml + xt[j1] * mr
                ws = wt[i0] * ml + wt[i1] * mr
                work.append((i0, i1, j0, j1, mm(xs, pair, NT), mm(ws, pair)))
            for i0, i1, j0, j1, yv, zv in work:
                ya[i0] += jnp.where(isl, yv, 0.0)
                ya[i1] += jnp.where(isl, 0.0, yv)
                za[j0] += jnp.where(isl, zv, 0.0)
                za[j1] += jnp.where(isl, 0.0, zv)
            return carry
        lax.fori_loop(0, steps, step, 0)

    unroll = 4
    run(s_ref, xc, wc, yc, zc, o_row, o_col, True, (live + 2 * unroll - 1) // (2 * unroll), unroll)
    run(d_ref, xp, wp, yn, zn, n_row, n_col, False, nears // (2 * unroll), unroll)

    def fold(acc, at):
        a, b = acc[at], acc[at + 1]
        return jnp.where(isl, a + pltpu.roll(a, half, 1), b + pltpu.roll(b, half, 1))

    def out_y(i, carry):
        for m in range(packs):
            y_ref[i, 0, m] = fold(yc, 2 * (i * packs + m)).astype(y_ref.dtype)
            y_ref[i, 1, m] = fold(yn, 2 * (i * packs + m)).astype(y_ref.dtype)
        return carry

    def out_z(i, carry):
        for m in range(packs):
            z_ref[i, m] = fold(zc, 2 * (i * packs + m)).astype(z_ref.dtype)
        return carry

    def out_n(i, carry):
        for m in range(packs):
            n_ref[i, m] = fold(zn, 2 * (i * packs + m)).astype(n_ref.dtype)
        return carry

    lax.fori_loop(0, cols, out_y, 0)
    lax.fori_loop(0, rows, out_z, 0)
    lax.fori_loop(0, 3, out_n, 0)


def down_kernel(rows, cols, y_ref, z_ref, n_ref, n0_ref, n2_ref, order_ref, u_ref, v_ref, eu_ref, ev_ref, fu_ref, fv_ref,
                s_ref, yo_ref, zo_ref, y_in, z1_in, z1_out, z2_in, zn_in, nodes, y_sem, z1_sem, z2_sem, n_sem):
    _, packs, q, wide = z_ref.shape
    half = wide // 2
    deep, inner = grid_of(rows)
    dev_count = rows * cols
    r = lax.axis_index("row")
    c = lax.axis_index("col")
    me = r * cols + c
    zi = r // inner
    xi = lax.rem(r, inner)
    bar = greet(rows, cols, r, c)
    ml, mr = left_mask(half, BF)
    isl = lax.broadcasted_iota(jnp.int32, (q, wide), 1) < half
    hot = one_hot(order_ref, me * order_ref.shape[1])
    pl.semaphore_wait(bar, rows + cols - 2)
    first = {}
    for d in list(range(1, deep)) + [0]:
        to = lax.rem(zi + d, deep) * inner
        first[d] = []
        for e in range(1, inner):
            peer = lax.rem(xi + e, inner)
            first[d].append(
                push(z_ref.at[to + peer], z1_in.at[d, e - 1], z1_sem, (d, e - 1), "row", zi * inner + peer)
            )
    near = [
        push(n_ref.at[0], zn_in.at[0], n_sem, (0,), "row", lax.rem(r + rows - 1, rows)),
        push(n_ref.at[2], zn_in.at[1], n_sem, (1,), "row", lax.rem(r + 1, rows)),
    ]
    y_copies = []
    for d in range(1, cols):
        peer = lax.rem(c + d, cols)
        y_copies.append(push(y_ref.at[peer], y_in.at[d - 1], y_sem, (d - 1,), "col", peer))

    second = []
    for d in range(1, deep):
        for copy in first[d]:
            copy.wait_recv()
        to = lax.rem(zi + d, deep) * inner + xi
        for m in range(packs):
            total = z_ref[to, m].astype(F32)
            for e in range(inner - 1):
                total = total + z1_in[d, e, m].astype(F32)
            z1_out[d - 1, m] = total.astype(BF)
        second.append(push(z1_out.at[d - 1], z2_in.at[d - 1], z2_sem, (d - 1,), "row", to))

    levels = dev_count.bit_length() - 1
    starts = []
    at = 0
    vals = None
    for level in range(levels):
        if level == 0:
            vals = [n0_ref[i].astype(F32) for i in range(cols)]
            split = r
        elif cols >> level == 1:
            vals = [n2_ref[i].astype(F32) for i in range(rows)]
            split = 0
        starts.append((at, c >> level if cols >> level > 1 else me >> level))
        for i, v in enumerate(vals):
            nodes[at + i] = v
        at += len(vals)
        off = dev_count - (dev_count >> level)
        count = len(vals) // 2
        if level < levels - 1 and count * 2 == len(vals) and not (cols >> level == 2):
            vals = [
                combine(
                    vals[2 * i],
                    vals[2 * i + 1],
                    chunk_at(fv_ref, off + split * count + i, wide),
                    chunk_at(fu_ref, off + split * count + i, wide),
                    ml, mr, isl, half,
                ).astype(F32)
                for i in range(count)
            ]

    lane_half = (lax.broadcasted_iota(jnp.int32, (q, wide), 1) >= half).astype(jnp.int32)

    def turned(v, chunk, side):
        return mm2(jnp.where(lane_half == side, v, 0.0), jnp.concatenate([chunk, chunk], axis=0), NT)

    y_down = z_down = None
    for level in range(levels - 1, -1, -1):
        start, local = starts[level]
        own = me >> level
        side = lax.rem(own, 2)
        sib = nodes[start + local + 1 - 2 * lax.rem(local, 2)]
        rolled = pltpu.roll(sib, half, 1)
        xs = jnp.where(isl, sib, rolled)
        ws = jnp.where(isl, rolled, 0.0).astype(BF)
        at = dev_count - (dev_count >> level) + own // 2
        cup = chunk_at(s_ref, at, wide)
        dup = jnp.concatenate([cup, cup], axis=0)
        y_term = mm(jnp.where(lane_half == side, xs, 0.0).astype(BF), dup, NT)
        z_raw = jnp.where(lane_half == 1 - side, mm(ws, dup), 0.0)
        z_term = z_raw + pltpu.roll(z_raw, half, 1)
        if level < levels - 1:
            y_term = y_term + turned(y_down, chunk_at(fu_ref, at, wide), side)
            z_term = z_term + turned(z_down, chunk_at(fv_ref, at, wide), side)
        y_down, z_down = y_term, z_term

    perms = []
    for flip, (down, b_ref, e_ref) in enumerate(((y_down, u_ref, eu_ref), (z_down, v_ref, ev_ref))):
        if flip == 0:
            for copy in y_copies:
                copy.wait_recv()
        else:
            for copy in first[0] + second + near:
                copy.wait_recv()
        parts = []
        for m in range(packs):
            cs = slice(m * wide, (m + 1) * wide)
            if flip == 0:
                coef, raw = y_ref[c, 0, m].astype(F32), y_ref[c, 1, m].astype(F32)
                for d in range(cols - 1):
                    coef = coef + y_in[d, 0, m].astype(F32)
                    raw = raw + y_in[d, 1, m].astype(F32)
            else:
                coef, raw = z_ref[r, m].astype(F32), n_ref[1, m].astype(F32)
                for e in range(inner - 1):
                    coef = coef + z1_in[0, e, m].astype(F32)
                for d in range(deep - 1):
                    coef = coef + z2_in[d, m].astype(F32)
                for k in range(2):
                    raw = raw + zn_in[k, m].astype(F32)
            leaf = (coef + mm2(down, diag2(e_ref[:, cs], ml, mr), NT)).astype(BF)
            parts.append((mm(leaf, diag2(b_ref[:, cs], ml, mr)) + raw).astype(BF))
        perms.append(jnp.concatenate(parts, axis=1))
    out = mm(jnp.concatenate(perms, axis=0), hot, NT).astype(BF)
    yo_ref[...] = out[:q]
    zo_ref[...] = out[q:]
    for copies in (*first.values(), second, near, y_copies):
        for copy in copies:
            copy.wait_send()


def per_device(
    x_vectors,
    w_vectors,
    order,
    ubasis,
    vbasis,
    leaf_up_u,
    leaf_up_v,
    coupling,
    coupling_pairs,
    coupling_count,
    near_blocks,
    near_pairs,
    transfer_u,
    transfer_v,
    upper_coupling,
):
    q, piece = x_vectors.shape
    rank = ubasis.shape[0]
    leaves = leaf_up_u.shape[1] // rank
    packs = leaves // 2
    wide = 2 * rank
    rows = lax.axis_size("row")
    cols = lax.axis_size("col")
    deep, inner = grid_of(rows)
    my_row = lax.axis_index("row")
    row_base = my_row * cols * leaves
    order2 = order.reshape(1, piece)

    def shape(*lead):
        return jax.ShapeDtypeStruct((*lead, q, wide), BF)

    def buf(*lead, dtype=BF):
        return pltpu.VMEM((*lead, q, wide), dtype)

    def sems(*lead):
        return pltpu.SemaphoreType.DMA((2, *lead))

    def params(cid=None):
        if cid is None:
            return pltpu.CompilerParams(vmem_limit_bytes=VLIMIT)
        return pltpu.CompilerParams(vmem_limit_bytes=VLIMIT, collective_id=cid, has_side_effects=True)

    x_all, x_pts, w_all, n0, n2 = pl.pallas_call(
        functools.partial(up_kernel, rows, cols),
        out_shape=(shape(rows, packs), shape(3, packs), shape(cols, 2, packs), shape(cols), shape(rows)),
        in_specs=[VMEM] * 9,
        out_specs=(VMEM,) * 5,
        scratch_shapes=[
            sems(cols - 1),
            sems(rows - 1),
            sems(deep - 1),
            sems(deep, inner - 1),
            sems(2),
            sems(cols - 1),
        ],
        compiler_params=params(0),
    )(x_vectors, w_vectors, order2, vbasis, ubasis, leaf_up_v, leaf_up_u, transfer_u, transfer_v)
    tiles = near_pairs[1] // leaves // cols
    ids = jnp.concatenate(
        [
            coupling_pairs[0] - row_base,
            coupling_pairs[1] // leaves // cols * leaves + coupling_pairs[1] % leaves,
            near_pairs[0] - row_base,
            (tiles - my_row + rows + 1) % rows * leaves + near_pairs[1] % leaves,
            coupling_count,
        ]
    )
    y_part, z_part, n_part = pl.pallas_call(
        slot_kernel,
        out_shape=(shape(cols, 2, packs), shape(rows, packs), shape(3, packs)),
        in_specs=[SMEM] + [VMEM] * 5,
        out_specs=(VMEM,) * 3,
        scratch_shapes=[
            buf(rows * leaves),
            buf(3 * leaves),
            buf(cols * leaves),
            buf(cols * leaves),
            buf(cols * leaves, dtype=F32),
            buf(cols * leaves, dtype=F32),
            buf(rows * leaves, dtype=F32),
            buf(3 * leaves, dtype=F32),
        ],
        compiler_params=params(),
    )(ids, x_all, x_pts, w_all, coupling, near_blocks)
    return pl.pallas_call(
        functools.partial(down_kernel, rows, cols),
        out_shape=(jax.ShapeDtypeStruct((q, piece), BF),) * 2,
        in_specs=[VMEM] * 13,
        out_specs=(VMEM,) * 2,
        scratch_shapes=[
            buf(cols - 1, 2, packs),
            buf(deep, inner - 1, packs),
            buf(deep - 1, packs),
            buf(deep - 1, packs),
            buf(2, packs),
            buf(2 * (rows + cols), dtype=F32),
            sems(cols - 1),
            sems(deep, inner - 1),
            sems(deep - 1),
            sems(2),
        ],
        compiler_params=params(1),
    )(
        y_part, z_part, n_part, n0, n2, order2, ubasis, vbasis, leaf_up_u, leaf_up_v,
        transfer_u, transfer_v, upper_coupling,
    )


def solution(mesh):
    both = P(None, ("row", "col"))
    flat = P(("row", "col"))
    return jax.shard_map(
        per_device,
        mesh=mesh,
        in_specs=(both, both, flat, both, both, both, both, both, both, flat, both, both, P(), P(), P()),
        out_specs=(both, both),
        check_vma=False,
    )
```

time: 252 us -> 97 us (0.38)
  waiting for transfers between devices: 174 us -> 0 us
  Pallas kernels: 37.8 us -> 90.2 us
  between operations: 14.5 us -> 1.33 us
  starting transfers between devices: 12.1 us -> 0 us
  matrix products: 9.84 us -> 0 us
    reduce_scatter x2 -> x0, waiting for transfers between devices: 96.4 us -> none  [the longest x1 91.9 us: per_device(): z_own = lax.psum_scatter(z_part, 'row', scatter_dimension=0, tiled=False)]
    all_gather x2 -> x0, waiting for transfers between devices: 67.1 us -> none  [the longest x1 51.2 us: per_device(): x_all = lax.all_gather(x_out, 'row', axis=0)]
    pallas_call x3, Pallas kernels: 37.8 us -> 90.2 us  [the longest x1 33.8 us: per_device(): pl.pallas_call(functools.partial(down_kernel, rows, cols), out_shape=(jax...]
    ppermute x5 -> x0, starting transfers between devices: 11.9 us -> none  [from_partner(): return lax.ppermute(block, axis, route)]
    ppermute x5 -> x0, waiting for transfers between devices: 10 us -> none  [from_partner(): return lax.ppermute(block, axis, route)]
    dot_general x42 -> x0, matrix products: 9.84 us -> none  [mm(): return lax.dot_general(a, b, dims, preferred_element_type=F32)]
  transfers between devices with their start and end apart: 9 -> 0, of which waited for: 9 -> 0; matrix products, arithmetic and copies ran while one was open for 5% -> 0% of each run, Pallas kernels for 0% -> 0%
where the time goes in v1:
time: 97 us; the launch traced here: 96.3 us
  Pallas kernels  90.2 us (93%)
  local copies, waits for them, and re-layouts  3.16 us (3%)
  other arithmetic  1.59 us (2%)
  between operations  1.33 us (1%)
    pallas_call x1, Pallas kernels, per_device(): pl.pallas_call(functools.partial(down_kernel, rows, cols), out_shape=(jax...  33.8 us
    pallas_call x1, Pallas kernels, per_device(): pl.pallas_call(functools.partial(up_kernel, rows, cols), out_shape=(shape...  29.2 us
    pallas_call x1, Pallas kernels, per_device(): pl.pallas_call(slot_kernel, out_shape=(shape(cols, 2, packs), shape(rows,...  27.2 us
    unnamed x6, local copies, waits for them, and re-layouts  3.15 us

profile of v1, /device:TPU:0, one launch (start us, length us, event | category | flops | bytes accessed | tf_op | source)
XLA Modules:
  0.0 96.3 jit_solution(5323448713724748305)
XLA Ops:
  1.3 0.8 fusion.9
  2.0 0.8 fusion.8
  2.9 0.0 copy-start
  2.9 29.2 %shard_map.158 = (bf16[8,8,64,128]{3,2,1,0:T(8,128)(2,1)}, bf16[3,8,64,128]{3,2,1,0:T(8,128)(2,1)}, bf16[4,2,8,64,128]{4,3,2,1,0:T(8,128)(2,1)}, bf16[4,64,128]{2,1,0:T(8,128)(2,1)}, bf16[8,64,128]{2,1,0:T(8,128)(2,1)}) custom-call(bf16[64,1024]{1,0:T(8,128)(2,1)} %x_ref.1, bf16[64,1024]{1,0:T(8,128)(2,1)} %w_ref.1, s32[1,1024]{1,0:T(1,128)} %bitcast.5, ...), custom_call_target="tpu_custom_call" | custom-call | tf_op jit(solution)/shard_map/pallas_call | solution.py:444
  32.2 0.0 copy-done
  32.2 27.2 %shard_map.159 = (bf16[4,2,8,64,128]{4,3,2,1,0:T(8,128)(2,1)}, bf16[8,8,64,128]{3,2,1,0:T(8,128)(2,1)}, bf16[3,8,64,128]{3,2,1,0:T(8,128)(2,1)}) custom-call(s32[1537]{0:T(1024)} %copy-done, bf16[8,8,64,128]{3,2,1,0:T(8,128)(2,1)} %get-tuple-element.10.x_ref, bf16[3,8,64,128]{3,2,1,0:T(8,128)(2,1)} %get-tuple-element.11.p_ref, ...), custom_call_target="tpu_custom_call" | custom-call | tf_op jit(solution)/shard_map/pallas_call | solution.py:469
  59.4 33.8 %shard_map.160 = (bf16[64,1024]{1,0:T(8,128)(2,1)}, bf16[64,1024]{1,0:T(8,128)(2,1)}) custom-call(bf16[4,2,8,64,128]{4,3,2,1,0:T(8,128)(2,1)} %get-tuple-element.13.y_ref, bf16[8,8,64,128]{3,2,1,0:T(8,128)(2,1)} %get-tuple-element.14.z_ref, bf16[3,8,64,128]{3,2,1,0:T(8,128)(2,1)} %get-tuple-element.15.n_ref, bf16[4,64,128]{2,1,0:T(8,128)(2,1)} %get-tuple-element.16.n0_ref, ...), custom_call_target="tpu_custom_call" | custom-call | tf_op jit(solution)/shard_map/pallas_call | solution.py:486
  93.2 1.6 %copy.25 = bf16[64,1024]{1,0:T(8,128)(2,1)} copy(bf16[64,1024]{1,0:T(8,128)(2,1)} %get-tuple-element.24) | data formatting | bytes 262144
  94.7 1.6 %copy.26 = bf16[64,1024]{1,0:T(8,128)(2,1)} copy(bf16[64,1024]{1,0:T(8,128)(2,1)} %get-tuple-element.25) | data formatting | bytes 262144
  (6 shorter events, 0.1 us)
Async XLA Ops:
  2.9 29.3 %copy-start = (s32[1537]{0:T(1024)}, s32[1537]{0:T(1024)S(1)}, u32[]{:S(2)}) copy-start(s32[1537]{0:T(1024)S(1)} %constant_dynamic-update-slice_fusion.ids_ref) | copy-start | bytes 18448

commit v2 on v1

--- a/solution.py
+++ b/solution.py
@@ -13,7 +13,6 @@
 SMEM = pl.BlockSpec(memory_space=pltpu.SMEM)
 NN = (((1,), (0,)), ((), ()))
 NT = (((1,), (1,)), ((), ()))
-VLIMIT = 60 * 1024 * 1024
 
 
 def mm(a, b, dims=NN):
@@ -27,6 +26,27 @@
 
 def diag2(v, ml, mr):
     return jnp.concatenate([v * ml, v * mr], axis=0)
+
+
+def swap2(a, b, isl, half):
+    return jnp.where(isl, a, pltpu.roll(b, half, 1)), jnp.where(isl, pltpu.roll(a, half, 1), b)
+
+
+def split_leaves(v, isl, half):
+    h = v.shape[0] // 2
+    return swap2(v[:h], v[h:], isl, half)
+
+
+def join_leaves(a, b, isl, half):
+    return jnp.concatenate(swap2(a, b, isl, half), axis=0)
+
+
+def quot(v, n):
+    return lax.shift_right_logical(v, n.bit_length() - 1) if n & (n - 1) == 0 else lax.div(v, n)
+
+
+def mod(v, n):
+    return lax.bitwise_and(v, n - 1) if n & (n - 1) == 0 else lax.rem(v, n)
 
 
 def split2(v):
@@ -87,7 +107,7 @@
 def up_kernel(rows, cols, x_ref, w_ref, order_ref, v_ref, u_ref, ev_ref, eu_ref, fu_ref, fv_ref,
               xc_ref, xp_ref, wa_ref, n0_ref, n2_ref, na_sem, nb_sem, z_sem, x_sem, p_sem, w_sem):
     q, n = x_ref.shape
-    packs = xc_ref.shape[1]
+    packs = xc_ref.shape[1] // 2
     wide = xc_ref.shape[3]
     half = wide // 2
     deep, inner = grid_of(rows)
@@ -99,21 +119,27 @@
     ml, mr = left_mask(half, BF)
     isl = lax.broadcasted_iota(jnp.int32, (q, wide), 1) < half
     hot = one_hot(order_ref, (r * cols + c) * n)
-    both = mm(jnp.concatenate([x_ref[...], w_ref[...]], axis=0), hot).astype(BF)
+    low = lax.broadcasted_iota(jnp.int32, (q // 2, wide), 1) < half
+    both = mm(jnp.concatenate([x_ref[...], w_ref[...]], axis=0), hot)
     folds = []
     for side, (b_ref, e_ref) in enumerate(((v_ref, ev_ref), (u_ref, eu_ref))):
-        pts = both[side * q:(side + 1) * q]
+        pts = both[side * q:(side + 1) * q].astype(BF)
         node = jnp.zeros((q, wide), F32)
         for m in range(packs):
             cs = slice(m * wide, (m + 1) * wide)
             pm = pts[:, cs]
-            cm = mm(pm, diag2(b_ref[:, cs], ml, mr), NT).astype(BF)
-            if side == 0:
-                xc_ref[r, m] = cm
-                xp_ref[1, m] = pm
-            else:
-                wa_ref[c, 0, m] = cm
-                wa_ref[c, 1, m] = pm
+            cf = mm(pm, diag2(b_ref[:, cs], ml, mr), NT)
+            cm = cf.astype(BF)
+            c_leaves = split_leaves(cf, low, half)
+            p_leaves = split_leaves(both[side * q:(side + 1) * q, cs], low, half)
+            for e in range(2):
+                ce, pe = c_leaves[e].astype(BF), p_leaves[e].astype(BF)
+                if side == 0:
+                    xc_ref[r, 2 * m + e] = ce
+                    xp_ref[1, 2 * m + e] = pe
+                else:
+                    wa_ref[c, 0, 2 * m + e] = ce
+                    wa_ref[c, 1, 2 * m + e] = pe
             node = node + mm(cm, diag2(e_ref[:, cs], ml, mr))
         folds.append(node + pltpu.roll(node, half, 1))
     n0_ref[c] = jnp.where(isl, folds[0], folds[1]).astype(BF)
@@ -167,95 +193,83 @@
         copy.wait_send()
 
 
-def slot_kernel(ids_ref, x_ref, p_ref, w_ref, s_ref, d_ref, y_ref, z_ref, n_ref, xc, xp, wc, wp, yc, yn, zc, zn):
-    rows, packs, q, wide = x_ref.shape
-    cols = w_ref.shape[0]
+def slot_kernel(rows, cols, cp_ref, np_ref, live_ref, x_ref, p_ref, w_ref, s_ref, d_ref, y_ref, z_ref, n_ref, ya, zc, zn):
+    leaves, _, wide = x_ref.shape[1:]
     half = wide // 2
     ml, mr = left_mask(half, BF)
-    slots = s_ref.shape[1] // half
-    nears = d_ref.shape[1] // half
-    o_row, o_col, n_row, n_col = 0, slots, 2 * slots, 2 * slots + nears
-    live = ids_ref[2 * slots + 2 * nears]
-    isl = lax.broadcasted_iota(jnp.int32, (q, wide), 1) < half
+    slots = cp_ref.shape[1]
+    nears = np_ref.shape[1]
+    live = live_ref[0]
+    my_row = lax.axis_index("row")
+    row_base = my_row * cols * leaves
     lane = lax.broadcasted_iota(jnp.int32, (1, wide), 1)
-    for acc in (yc, yn, zc, zn):
-        def clear(i, carry, acc=acc):
+
+    def clear(acc):
+        def one(i, carry):
             acc[i] = jnp.zeros(acc.shape[1:], F32)
             return carry
-        lax.fori_loop(0, acc.shape[0], clear, 0)
-
-    def widen(src, table, at):
-        v = src[...].astype(F32)
-        r = pltpu.roll(v, half, 1)
-        table[at] = jnp.where(isl, v, r).astype(BF)
-        table[at + 1] = jnp.where(isl, r, v).astype(BF)
-
-    def fill_x(i, carry):
-        for m in range(packs):
-            widen(x_ref.at[i, m], xc, 2 * (i * packs + m))
-        return carry
-
-    def fill_w(i, carry):
-        for m in range(packs):
-            widen(w_ref.at[i, 0, m], wc, 2 * (i * packs + m))
-            widen(w_ref.at[i, 1, m], wp, 2 * (i * packs + m))
-        return carry
-
-    lax.fori_loop(0, rows, fill_x, 0)
-    lax.fori_loop(0, cols, fill_w, 0)
-    for k in range(3):
-        for m in range(packs):
-            widen(p_ref.at[k, m], xp, 2 * (k * packs + m))
-
-    def run(mat, xt, wt, ya, za, row_at, col_at, masked, steps, unroll):
+        lax.fori_loop(0, acc.shape[0], one, 0)
+
+    clear(ya.at[0])
+    clear(ya.at[1])
+    clear(zc)
+    clear(zn)
+
+    def run(pairs, mat, kind, first, last, unroll, masked):
+        near = kind == 1
+
         def step(g, carry):
             work = []
             for k in range(unroll):
                 p = g * unroll + k
-                i0, i1 = ids_ref[row_at + 2 * p], ids_ref[row_at + 2 * p + 1]
-                j0, j1 = ids_ref[col_at + 2 * p], ids_ref[col_at + 2 * p + 1]
                 blk = mat[:, pl.ds(pl.multiple_of(p * wide, wide), wide)]
-                if masked:
-                    left_ok = jnp.where(2 * p < live, 1.0, 0.0)
-                    right_ok = jnp.where(2 * p + 1 < live, 1.0, 0.0)
-                    a = jnp.where(lane < half, left_ok, 0.0).astype(BF)
-                    b = jnp.where(lane < half, 0.0, right_ok).astype(BF)
-                else:
-                    a, b = ml, mr
-                pair = jnp.concatenate([blk * a, blk * b], axis=0)
-                xs = xt[j0] * ml + xt[j1] * mr
-                ws = wt[i0] * ml + wt[i1] * mr
-                work.append((i0, i1, j0, j1, mm(xs, pair, NT), mm(ws, pair)))
-            for i0, i1, j0, j1, yv, zv in work:
-                ya[i0] += jnp.where(isl, yv, 0.0)
-                ya[i1] += jnp.where(isl, 0.0, yv)
-                za[j0] += jnp.where(isl, zv, 0.0)
-                za[j1] += jnp.where(isl, 0.0, zv)
+                alt = jnp.concatenate([blk[:, half:], blk[:, :half]], axis=1)
+                for e in range(2):
+                    b = 2 * p + e
+                    i = pairs[0, b] - row_base
+                    l = pairs[1, b]
+                    group = quot(l, cols * leaves)
+                    leaf = mod(l, leaves)
+                    if near:
+                        group = mod(group - my_row + (rows + 1), rows)
+                    a_l, a_r = ml, mr
+                    if masked:
+                        ok = jnp.where(b < live, 1.0, 0.0)
+                        a_l = jnp.where(lane < half, ok, 0.0).astype(BF)
+                        a_r = jnp.where(lane < half, 0.0, ok).astype(BF)
+                    one, two = (alt, blk) if e else (blk, alt)
+                    both = jnp.concatenate([one * a_l, two * a_r], axis=0)
+                    xv = p_ref[group, leaf] if near else x_ref[group, leaf]
+                    wv = w_ref[quot(i, leaves), kind, mod(i, leaves)]
+                    j = group * leaves + leaf
+                    work.append((i, j, mm(xv, both, NT), mm(wv, both)))
+            zacc = zn if near else zc
+            for i, j, yv, zv in work:
+                ya[kind, i] += yv
+                zacc[j] += zv
             return carry
-        lax.fori_loop(0, steps, step, 0)
+        lax.fori_loop(first, last, step, 0)
 
     unroll = 4
-    run(s_ref, xc, wc, yc, zc, o_row, o_col, True, (live + 2 * unroll - 1) // (2 * unroll), unroll)
-    run(d_ref, xp, wp, yn, zn, n_row, n_col, False, nears // (2 * unroll), unroll)
-
-    def fold(acc, at):
-        a, b = acc[at], acc[at + 1]
-        return jnp.where(isl, a + pltpu.roll(a, half, 1), b + pltpu.roll(b, half, 1))
+    full = quot(live, 2 * unroll)
+    run(cp_ref, s_ref, 0, 0, full, unroll, False)
+    run(cp_ref, s_ref, 0, full, quot(live + 2 * unroll - 1, 2 * unroll), unroll, True)
+    run(np_ref, d_ref, 1, 0, nears // (2 * unroll), unroll, False)
 
     def out_y(i, carry):
-        for m in range(packs):
-            y_ref[i, 0, m] = fold(yc, 2 * (i * packs + m)).astype(y_ref.dtype)
-            y_ref[i, 1, m] = fold(yn, 2 * (i * packs + m)).astype(y_ref.dtype)
+        for t in range(2):
+            for m in range(leaves):
+                y_ref[i, t, m] = ya[t, i * leaves + m].astype(BF)
         return carry
 
     def out_z(i, carry):
-        for m in range(packs):
-            z_ref[i, m] = fold(zc, 2 * (i * packs + m)).astype(z_ref.dtype)
+        for m in range(leaves):
+            z_ref[i, m] = zc[i * leaves + m].astype(BF)
         return carry
 
     def out_n(i, carry):
-        for m in range(packs):
-            n_ref[i, m] = fold(zn, 2 * (i * packs + m)).astype(n_ref.dtype)
+        for m in range(leaves):
+            n_ref[i, m] = zn[i * leaves + m].astype(BF)
         return carry
 
     lax.fori_loop(0, cols, out_y, 0)
@@ -264,9 +278,11 @@
 
 
 def down_kernel(rows, cols, y_ref, z_ref, n_ref, n0_ref, n2_ref, order_ref, u_ref, v_ref, eu_ref, ev_ref, fu_ref, fv_ref,
-                s_ref, yo_ref, zo_ref, y_in, z1_in, z1_out, z2_in, zn_in, nodes, y_sem, z1_sem, z2_sem, n_sem):
-    _, packs, q, wide = z_ref.shape
+                s_ref, o_ref, y_in, z1_in, z1_out, z2_in, zn_in, nodes, y_sem, z1_sem, z2_sem, n_sem):
+    _, leaves, q, wide = z_ref.shape
+    q = 2 * q
     half = wide // 2
+    low = lax.broadcasted_iota(jnp.int32, (q // 2, wide), 1) < half
     deep, inner = grid_of(rows)
     dev_count = rows * cols
     r = lax.axis_index("row")
@@ -302,7 +318,7 @@
         for copy in first[d]:
             copy.wait_recv()
         to = lax.rem(zi + d, deep) * inner + xi
-        for m in range(packs):
+        for m in range(leaves):
             total = z_ref[to, m].astype(F32)
             for e in range(inner - 1):
                 total = total + z1_in[d, e, m].astype(F32)
@@ -372,27 +388,29 @@
             for copy in first[0] + second + near:
                 copy.wait_recv()
         parts = []
-        for m in range(packs):
+        for m in range(leaves // 2):
             cs = slice(m * wide, (m + 1) * wide)
-            if flip == 0:
-                coef, raw = y_ref[c, 0, m].astype(F32), y_ref[c, 1, m].astype(F32)
-                for d in range(cols - 1):
-                    coef = coef + y_in[d, 0, m].astype(F32)
-                    raw = raw + y_in[d, 1, m].astype(F32)
-            else:
-                coef, raw = z_ref[r, m].astype(F32), n_ref[1, m].astype(F32)
-                for e in range(inner - 1):
-                    coef = coef + z1_in[0, e, m].astype(F32)
-                for d in range(deep - 1):
-                    coef = coef + z2_in[d, m].astype(F32)
-                for k in range(2):
-                    raw = raw + zn_in[k, m].astype(F32)
+            sums = []
+            for n in (2 * m, 2 * m + 1):
+                if flip == 0:
+                    coef, raw = y_ref[c, 0, n].astype(F32), y_ref[c, 1, n].astype(F32)
+                    for d in range(cols - 1):
+                        coef = coef + y_in[d, 0, n].astype(F32)
+                        raw = raw + y_in[d, 1, n].astype(F32)
+                else:
+                    coef, raw = z_ref[r, n].astype(F32), n_ref[1, n].astype(F32)
+                    for e in range(inner - 1):
+                        coef = coef + z1_in[0, e, n].astype(F32)
+                    for d in range(deep - 1):
+                        coef = coef + z2_in[d, n].astype(F32)
+                    for k in range(2):
+                        raw = raw + zn_in[k, n].astype(F32)
+                sums.append((coef, raw))
+            coef, raw = (join_leaves(a, b, low, half) for a, b in zip(*sums))
             leaf = (coef + mm2(down, diag2(e_ref[:, cs], ml, mr), NT)).astype(BF)
             parts.append((mm(leaf, diag2(b_ref[:, cs], ml, mr)) + raw).astype(BF))
         perms.append(jnp.concatenate(parts, axis=1))
-    out = mm(jnp.concatenate(perms, axis=0), hot, NT).astype(BF)
-    yo_ref[...] = out[:q]
-    zo_ref[...] = out[q:]
+    o_ref[...] = mm(jnp.concatenate(perms, axis=0), hot, NT).astype(BF)
     for copies in (*first.values(), second, near, y_copies):
         for copy in copies:
             copy.wait_send()
@@ -418,18 +436,21 @@
     q, piece = x_vectors.shape
     rank = ubasis.shape[0]
     leaves = leaf_up_u.shape[1] // rank
-    packs = leaves // 2
     wide = 2 * rank
     rows = lax.axis_size("row")
     cols = lax.axis_size("col")
     deep, inner = grid_of(rows)
-    my_row = lax.axis_index("row")
-    row_base = my_row * cols * leaves
     order2 = order.reshape(1, piece)
+
+    def leaf_shape(*lead):
+        return jax.ShapeDtypeStruct((*lead, q // 2, wide), BF)
 
     def shape(*lead):
         return jax.ShapeDtypeStruct((*lead, q, wide), BF)
 
+    def leaf_buf(*lead, dtype=BF):
+        return pltpu.VMEM((*lead, q // 2, wide), dtype)
+
     def buf(*lead, dtype=BF):
         return pltpu.VMEM((*lead, q, wide), dtype)
 
@@ -438,12 +459,15 @@
 
     def params(cid=None):
         if cid is None:
-            return pltpu.CompilerParams(vmem_limit_bytes=VLIMIT)
-        return pltpu.CompilerParams(vmem_limit_bytes=VLIMIT, collective_id=cid, has_side_effects=True)
-
+            return pltpu.CompilerParams(vmem_limit_bytes=28 * 1024 * 1024)
+        return pltpu.CompilerParams(vmem_limit_bytes=24 * 1024 * 1024, collective_id=cid, has_side_effects=True)
+
+    cost = pl.CostEstimate(
+        flops=12 * q * rank * coupling.shape[1], bytes_accessed=128 * q * piece * rows, transcendentals=0
+    )
     x_all, x_pts, w_all, n0, n2 = pl.pallas_call(
         functools.partial(up_kernel, rows, cols),
-        out_shape=(shape(rows, packs), shape(3, packs), shape(cols, 2, packs), shape(cols), shape(rows)),
+        out_shape=(leaf_shape(rows, leaves), leaf_shape(3, leaves), leaf_shape(cols, 2, leaves), shape(cols), shape(rows)),
         in_specs=[VMEM] * 9,
         out_specs=(VMEM,) * 5,
         scratch_shapes=[
@@ -455,45 +479,32 @@
             sems(cols - 1),
         ],
         compiler_params=params(0),
+        cost_estimate=cost,
     )(x_vectors, w_vectors, order2, vbasis, ubasis, leaf_up_v, leaf_up_u, transfer_u, transfer_v)
-    tiles = near_pairs[1] // leaves // cols
-    ids = jnp.concatenate(
-        [
-            coupling_pairs[0] - row_base,
-            coupling_pairs[1] // leaves // cols * leaves + coupling_pairs[1] % leaves,
-            near_pairs[0] - row_base,
-            (tiles - my_row + rows + 1) % rows * leaves + near_pairs[1] % leaves,
-            coupling_count,
-        ]
-    )
     y_part, z_part, n_part = pl.pallas_call(
-        slot_kernel,
-        out_shape=(shape(cols, 2, packs), shape(rows, packs), shape(3, packs)),
-        in_specs=[SMEM] + [VMEM] * 5,
+        functools.partial(slot_kernel, rows, cols),
+        out_shape=(leaf_shape(cols, 2, leaves), leaf_shape(rows, leaves), leaf_shape(3, leaves)),
+        in_specs=[SMEM] * 3 + [VMEM] * 5,
         out_specs=(VMEM,) * 3,
         scratch_shapes=[
-            buf(rows * leaves),
-            buf(3 * leaves),
-            buf(cols * leaves),
-            buf(cols * leaves),
-            buf(cols * leaves, dtype=F32),
-            buf(cols * leaves, dtype=F32),
-            buf(rows * leaves, dtype=F32),
-            buf(3 * leaves, dtype=F32),
+            leaf_buf(2, cols * leaves, dtype=F32),
+            leaf_buf(rows * leaves, dtype=F32),
+            leaf_buf(3 * leaves, dtype=F32),
         ],
         compiler_params=params(),
-    )(ids, x_all, x_pts, w_all, coupling, near_blocks)
-    return pl.pallas_call(
+        cost_estimate=cost,
+    )(coupling_pairs, near_pairs, coupling_count, x_all, x_pts, w_all, coupling, near_blocks)
+    out = pl.pallas_call(
         functools.partial(down_kernel, rows, cols),
-        out_shape=(jax.ShapeDtypeStruct((q, piece), BF),) * 2,
+        out_shape=jax.ShapeDtypeStruct((2 * q, piece), BF),
         in_specs=[VMEM] * 13,
-        out_specs=(VMEM,) * 2,
+        out_specs=VMEM,
         scratch_shapes=[
-            buf(cols - 1, 2, packs),
-            buf(deep, inner - 1, packs),
-            buf(deep - 1, packs),
-            buf(deep - 1, packs),
-            buf(2, packs),
+            leaf_buf(cols - 1, 2, leaves),
+            leaf_buf(deep, inner - 1, leaves),
+            leaf_buf(deep - 1, leaves),
+            leaf_buf(deep - 1, leaves),
+            leaf_buf(2, leaves),
             buf(2 * (rows + cols), dtype=F32),
             sems(cols - 1),
             sems(deep, inner - 1),
@@ -501,10 +512,12 @@
             sems(2),
         ],
         compiler_params=params(1),
+        cost_estimate=cost,
     )(
         y_part, z_part, n_part, n0, n2, order2, ubasis, vbasis, leaf_up_u, leaf_up_v,
         transfer_u, transfer_v, upper_coupling,
     )
+    return out[:q], out[q:]
 
 
 def solution(mesh):

time: 97 us -> 105 us (1.082)
  local copies, waits for them, and re-layouts: 3.16 us -> 10.9 us
  other arithmetic: 1.59 us -> 0 us
  Pallas kernels: 90.2 us -> 91.5 us
    unnamed x6 -> x42, local copies, waits for them, and re-layouts: 3.15 us -> 10.2 us
    slice x2 -> x0, other arithmetic: 1.53 us -> none  [the longest x1 0.77 us: per_device(): coupling_pairs[1] // leaves // cols * leaves + coupling_pairs[1] % leaves]
    pallas_call x3, Pallas kernels: 90.2 us -> 91.5 us  [the longest x1 40.4 us: per_device(): pl.pallas_call(functools.partial(slot_kernel, rows, cols), out_shape=(lea...]
where the time goes in v2:
time: 105 us; the launch traced here: 104 us
  Pallas kernels  91.5 us (87%)
  local copies, waits for them, and re-layouts  10.9 us (10%)
  between operations  1.62 us (2%)
    pallas_call x1, Pallas kernels, per_device(): pl.pallas_call(functools.partial(slot_kernel, rows, cols), out_shape=(lea...  40.4 us
    pallas_call x1, Pallas kernels, per_device(): pl.pallas_call(functools.partial(up_kernel, rows, cols), out_shape=(leaf_...  26.2 us
    pallas_call x1, Pallas kernels, per_device(): pl.pallas_call(functools.partial(down_kernel, rows, cols), out_shape=jax....  25 us
    unnamed x42, local copies, waits for them, and re-layouts  10.2 us

profile of v2, /device:TPU:0, one launch (start us, length us, event | category | flops | bytes accessed | tf_op | source)
XLA Modules:
  0.0 104.1 jit_solution(17673367978043667675)
XLA Ops:
  0.6 0.0 copy-start.3
  0.6 0.0 copy-start.2
  0.7 0.0 copy-start
  1.5 0.0 copy-start.5
  1.5 1.4 %copy-done.5 = bf16[64,3840]{1,0:T(8,128)(2,1)S(1)} copy-done((bf16[64,3840]{1,0:T(8,128)(2,1)S(1)}, bf16[64,3840]{1,0:T(8,128)(2,1)}, u32[]{:S(2)}) %copy-start.5) | copy-done | bytes 491544
  2.9 0.0 copy-start.7
  2.9 1.0 copy-done.7
  3.9 0.0 copy-start.9
  3.9 0.9 copy-done.9
  4.8 0.0 copy-start.10
  4.9 0.9 copy-done.10
  5.8 0.0 copy-start.11
  5.8 0.9 copy-done.11
  6.7 0.0 copy-start.13
  6.7 0.9 copy-done.13
  7.6 0.0 copy-start.15
  7.6 0.9 copy-done.15
  8.5 0.0 copy-start.17
  8.5 0.9 copy-done.17
  9.4 0.0 copy-start.19
  9.4 0.7 copy-done.19
  10.1 26.2 %shard_map.158 = (bf16[8,16,32,128]{3,2,1,0:T(8,128)(2,1)S(1)}, bf16[3,16,32,128]{3,2,1,0:T(8,128)(2,1)S(1)}, bf16[4,2,16,32,128]{4,3,2,1,0:T(8,128)(2,1)S(1)}, ...) custom-call(bf16[64,1024]{1,0:T(8,128)(2,1)S(1)} %copy-done.9, bf16[64,1024]{1,0:T(8,128)(2,1)S(1)} %copy-done.10, ...), custom_call_target="tpu_custom_call" | custom-call | flops 1610612736 | bytes 67108864 | tf_op jit(solution)/shard_map/pallas_call | solution.py:468
  36.2 0.0 copy-done.3
  36.3 0.0 copy-done.2
  36.3 0.0 copy-done
  36.3 0.0 copy-start.1
  36.3 1.6 %copy-done.1 = bf16[64,16384]{1,0:T(8,128)(2,1)S(1)} copy-done((bf16[64,16384]{1,0:T(8,128)(2,1)S(1)}, bf16[64,16384]{1,0:T(8,128)(2,1)}, u32[]{:S(2)}) %copy-start.1) | copy-done | bytes 2097176
  37.9 0.0 copy-start.4
  37.9 0.0 copy-start.6
  37.9 0.0 copy-start.8
  37.9 0.0 copy-start.12
  37.9 0.0 copy-start.14
  37.9 0.0 copy-start.16
  37.9 0.0 copy-start.18
  37.9 0.0 copy-start.20
  37.9 40.4 %shard_map.159 = (bf16[4,2,16,32,128]{4,3,2,1,0:T(8,128)(2,1)S(1)}, bf16[8,16,32,128]{3,2,1,0:T(8,128)(2,1)S(1)}, bf16[3,16,32,128]{3,2,1,0:T(8,128)(2,1)S(1)}) custom-call(s32[2,512]{1,0:T(2,128)S(1)} %copy-done.2, s32[2,256]{1,0:T(2,128)S(1)} %copy-done.3, s32[1]{0:T(128)S(6)} %copy.17.live_ref, bf16[8,16,32,128]{3,2,1,0:T(8,128)(2,1)S(1)} %get-tuple-element.10.x_ref, ...), custom_call_target="tpu_custom_call" | custom-call | flops 1610612736 | bytes 67108864 | tf_op jit(solution)/shard_map/pallas_call | solution.py:484
  78.3 0.0 copy-done.4
  78.3 0.0 copy-done.6
  78.4 0.0 copy-done.8
  78.4 0.0 copy-done.12
  78.4 0.0 copy-done.14
  78.4 0.0 copy-done.16
  78.4 0.0 copy-done.18
  78.4 0.0 copy-done.20
  78.4 25.0 %shard_map.160 = bf16[128,1024]{1,0:T(8,128)(2,1)S(1)} custom-call(bf16[4,2,16,32,128]{4,3,2,1,0:T(8,128)(2,1)S(1)} %get-tuple-element.13.y_ref, bf16[8,16,32,128]{3,2,1,0:T(8,128)(2,1)S(1)} %get-tuple-element.14.z_ref, bf16[3,16,32,128]{3,2,1,0:T(8,128)(2,1)S(1)} %get-tuple-element.15.n_ref, bf16[4,64,128]{2,1,0:T(8,128)(2,1)S(1)} %get-tuple-element.16.n0_ref, ...), custom_call_target="tpu_custom_call" | custom-call | flops 1610612736 | bytes 67108864 | tf_op jit(solution)/shard_map/pallas_call | solution.py:497
  103.4 0.7 fusion
Async XLA Ops:
  0.6 35.6 %copy-start.3 = (s32[2,256]{1,0:T(2,128)S(1)}, s32[2,256]{1,0:T(2,128)}, u32[]{:S(2)}) copy-start(s32[2,256]{1,0:T(2,128)} %np_ref.1) | copy-start | bytes 6148
  0.6 35.6 %copy-start.2 = (s32[2,512]{1,0:T(2,128)S(1)}, s32[2,512]{1,0:T(2,128)}, u32[]{:S(2)}) copy-start(s32[2,512]{1,0:T(2,128)} %cp_ref.1) | copy-start | bytes 12292
  0.7 35.6 %copy-start = (bf16[64,32768]{1,0:T(8,128)(2,1)S(1)}, bf16[64,32768]{1,0:T(8,128)(2,1)}, u32[]{:S(2)}) copy-start(bf16[64,32768]{1,0:T(8,128)(2,1)} %s_ref.2) | copy-start | bytes 12582916
  1.5 1.5 %copy-start.5 = (bf16[64,3840]{1,0:T(8,128)(2,1)S(1)}, bf16[64,3840]{1,0:T(8,128)(2,1)}, u32[]{:S(2)}) copy-start(bf16[64,3840]{1,0:T(8,128)(2,1)} %fu_ref.3) | copy-start | bytes 1474564
  2.9 1.0 copy-start.7
  3.9 0.9 copy-start.9
  4.8 0.9 copy-start.10
  5.8 0.9 copy-start.11
  6.7 0.9 copy-start.13
  7.6 0.9 copy-start.15
  8.5 0.9 copy-start.17
  9.4 0.7 copy-start.19
  36.3 1.6 %copy-start.1 = (bf16[64,16384]{1,0:T(8,128)(2,1)S(1)}, bf16[64,16384]{1,0:T(8,128)(2,1)}, u32[]{:S(2)}) copy-start(bf16[64,16384]{1,0:T(8,128)(2,1)} %d_ref.1) | copy-start | bytes 6291460
  37.9 40.5 %copy-start.4 = (bf16[64,3968]{1,0:T(8,128)(2,1)S(1)}, bf16[64,3968]{1,0:T(8,128)(2,1)}, u32[]{:S(2)}) copy-start(bf16[64,3968]{1,0:T(8,128)(2,1)} %s_ref.3) | copy-start | bytes 1523716
  37.9 40.5 %copy-start.6 = (bf16[64,3840]{1,0:T(8,128)(2,1)S(1)}, bf16[64,3840]{1,0:T(8,128)(2,1)}, u32[]{:S(2)}) copy-start(bf16[64,3840]{1,0:T(8,128)(2,1)} %fu_ref.3) | copy-start | bytes 1474564
  37.9 40.5 %copy-start.8 = (bf16[64,3840]{1,0:T(8,128)(2,1)S(1)}, bf16[64,3840]{1,0:T(8,128)(2,1)}, u32[]{:S(2)}) copy-start(bf16[64,3840]{1,0:T(8,128)(2,1)} %fv_ref.3) | copy-start | bytes 1474564
  37.9 40.5 %copy-start.12 = (bf16[64,1024]{1,0:T(8,128)(2,1)S(1)}, bf16[64,1024]{1,0:T(8,128)(2,1)}, u32[]{:S(2)}) copy-start(bf16[64,1024]{1,0:T(8,128)(2,1)} %v_ref.3) | copy-start | bytes 393220
  37.9 40.5 %copy-start.14 = (bf16[64,1024]{1,0:T(8,128)(2,1)S(1)}, bf16[64,1024]{1,0:T(8,128)(2,1)}, u32[]{:S(2)}) copy-start(bf16[64,1024]{1,0:T(8,128)(2,1)} %u_ref.3) | copy-start | bytes 393220
  37.9 40.5 %copy-start.16 = (bf16[64,1024]{1,0:T(8,128)(2,1)S(1)}, bf16[64,1024]{1,0:T(8,128)(2,1)}, u32[]{:S(2)}) copy-start(bf16[64,1024]{1,0:T(8,128)(2,1)} %ev_ref.3) | copy-start | bytes 393220
  37.9 40.5 %copy-start.18 = (bf16[64,1024]{1,0:T(8,128)(2,1)S(1)}, bf16[64,1024]{1,0:T(8,128)(2,1)}, u32[]{:S(2)}) copy-start(bf16[64,1024]{1,0:T(8,128)(2,1)} %eu_ref.3) | copy-start | bytes 393220
  37.9 40.5 %copy-start.20 = (s32[1024]{0:T(1024)S(1)}, s32[1024]{0:T(1024)}, u32[]{:S(2)}) copy-start(s32[1024]{0:T(1024)} %param.17) | copy-start | bytes 12292

commit v3 on v1

--- a/solution.py
+++ b/solution.py
@@ -27,6 +27,14 @@
 
 def diag2(v, ml, mr):
     return jnp.concatenate([v * ml, v * mr], axis=0)
+
+
+def quot(v, n):
+    return lax.shift_right_logical(v, n.bit_length() - 1) if n & (n - 1) == 0 else lax.div(v, n)
+
+
+def mod(v, n):
+    return lax.bitwise_and(v, n - 1) if n & (n - 1) == 0 else lax.rem(v, n)
 
 
 def split2(v):
@@ -167,15 +175,16 @@
         copy.wait_send()
 
 
-def slot_kernel(ids_ref, x_ref, p_ref, w_ref, s_ref, d_ref, y_ref, z_ref, n_ref, xc, xp, wc, wp, yc, yn, zc, zn):
+def slot_kernel(cp_ref, np_ref, live_ref, x_ref, p_ref, w_ref, s_ref, d_ref, y_ref, z_ref, n_ref, xc, xp, wc, wp, yc, yn, zc, zn):
     rows, packs, q, wide = x_ref.shape
     cols = w_ref.shape[0]
     half = wide // 2
     ml, mr = left_mask(half, BF)
-    slots = s_ref.shape[1] // half
-    nears = d_ref.shape[1] // half
-    o_row, o_col, n_row, n_col = 0, slots, 2 * slots, 2 * slots + nears
-    live = ids_ref[2 * slots + 2 * nears]
+    leaves = 2 * packs
+    nears = np_ref.shape[1]
+    live = live_ref[0]
+    my_row = lax.axis_index("row")
+    row_base = my_row * cols * leaves
     isl = lax.broadcasted_iota(jnp.int32, (q, wide), 1) < half
     lane = lax.broadcasted_iota(jnp.int32, (1, wide), 1)
     for acc in (yc, yn, zc, zn):
@@ -185,10 +194,10 @@
         lax.fori_loop(0, acc.shape[0], clear, 0)
 
     def widen(src, table, at):
-        v = src[...].astype(F32)
-        r = pltpu.roll(v, half, 1)
-        table[at] = jnp.where(isl, v, r).astype(BF)
-        table[at + 1] = jnp.where(isl, r, v).astype(BF)
+        v = src[...]
+        r = jnp.concatenate([v[:, half:], v[:, :half]], axis=1)
+        table[at] = v * ml + r * mr
+        table[at + 1] = r * ml + v * mr
 
     def fill_x(i, carry):
         for m in range(packs):
@@ -207,13 +216,20 @@
         for m in range(packs):
             widen(p_ref.at[k, m], xp, 2 * (k * packs + m))
 
-    def run(mat, xt, wt, ya, za, row_at, col_at, masked, steps, unroll):
+    def place(pairs, b, near):
+        leaf = pairs[1, b]
+        group = quot(leaf, cols * leaves)
+        if near:
+            group = mod(group - my_row + (rows + 1), rows)
+        return pairs[0, b] - row_base, group * leaves + mod(leaf, leaves)
+
+    def run(pairs, mat, xt, wt, ya, za, near, masked, first, last, unroll):
         def step(g, carry):
             work = []
             for k in range(unroll):
                 p = g * unroll + k
-                i0, i1 = ids_ref[row_at + 2 * p], ids_ref[row_at + 2 * p + 1]
-                j0, j1 = ids_ref[col_at + 2 * p], ids_ref[col_at + 2 * p + 1]
+                i0, j0 = place(pairs, 2 * p, near)
+                i1, j1 = place(pairs, 2 * p + 1, near)
                 blk = mat[:, pl.ds(pl.multiple_of(p * wide, wide), wide)]
                 if masked:
                     left_ok = jnp.where(2 * p < live, 1.0, 0.0)
@@ -232,11 +248,14 @@
                 za[j0] += jnp.where(isl, zv, 0.0)
                 za[j1] += jnp.where(isl, 0.0, zv)
             return carry
-        lax.fori_loop(0, steps, step, 0)
+        lax.fori_loop(first, last, step, 0)
 
     unroll = 4
-    run(s_ref, xc, wc, yc, zc, o_row, o_col, True, (live + 2 * unroll - 1) // (2 * unroll), unroll)
-    run(d_ref, xp, wp, yn, zn, n_row, n_col, False, nears // (2 * unroll), unroll)
+    full = quot(live, 2 * unroll)
+    most = quot(live + 2 * unroll - 1, 2 * unroll)
+    run(cp_ref, s_ref, xc, wc, yc, zc, False, False, 0, full, unroll)
+    run(cp_ref, s_ref, xc, wc, yc, zc, False, True, full, most, unroll)
+    run(np_ref, d_ref, xp, wp, yn, zn, True, False, 0, nears // (2 * unroll), unroll)
 
     def fold(acc, at):
         a, b = acc[at], acc[at + 1]
@@ -264,7 +283,7 @@
 
 
 def down_kernel(rows, cols, y_ref, z_ref, n_ref, n0_ref, n2_ref, order_ref, u_ref, v_ref, eu_ref, ev_ref, fu_ref, fv_ref,
-                s_ref, yo_ref, zo_ref, y_in, z1_in, z1_out, z2_in, zn_in, nodes, y_sem, z1_sem, z2_sem, n_sem):
+                s_ref, o_ref, y_in, z1_in, z1_out, z2_in, zn_in, nodes, y_sem, z1_sem, z2_sem, n_sem):
     _, packs, q, wide = z_ref.shape
     half = wide // 2
     deep, inner = grid_of(rows)
@@ -390,9 +409,7 @@
             leaf = (coef + mm2(down, diag2(e_ref[:, cs], ml, mr), NT)).astype(BF)
             parts.append((mm(leaf, diag2(b_ref[:, cs], ml, mr)) + raw).astype(BF))
         perms.append(jnp.concatenate(parts, axis=1))
-    out = mm(jnp.concatenate(perms, axis=0), hot, NT).astype(BF)
-    yo_ref[...] = out[:q]
-    zo_ref[...] = out[q:]
+    o_ref[...] = mm(jnp.concatenate(perms, axis=0), hot, NT).astype(BF)
     for copies in (*first.values(), second, near, y_copies):
         for copy in copies:
             copy.wait_send()
@@ -423,8 +440,6 @@
     rows = lax.axis_size("row")
     cols = lax.axis_size("col")
     deep, inner = grid_of(rows)
-    my_row = lax.axis_index("row")
-    row_base = my_row * cols * leaves
     order2 = order.reshape(1, piece)
 
     def shape(*lead):
@@ -456,20 +471,10 @@
         ],
         compiler_params=params(0),
     )(x_vectors, w_vectors, order2, vbasis, ubasis, leaf_up_v, leaf_up_u, transfer_u, transfer_v)
-    tiles = near_pairs[1] // leaves // cols
-    ids = jnp.concatenate(
-        [
-            coupling_pairs[0] - row_base,
-            coupling_pairs[1] // leaves // cols * leaves + coupling_pairs[1] % leaves,
-            near_pairs[0] - row_base,
-            (tiles - my_row + rows + 1) % rows * leaves + near_pairs[1] % leaves,
-            coupling_count,
-        ]
-    )
     y_part, z_part, n_part = pl.pallas_call(
         slot_kernel,
         out_shape=(shape(cols, 2, packs), shape(rows, packs), shape(3, packs)),
-        in_specs=[SMEM] + [VMEM] * 5,
+        in_specs=[SMEM] * 3 + [VMEM] * 5,
         out_specs=(VMEM,) * 3,
         scratch_shapes=[
             buf(rows * leaves),
@@ -482,12 +487,12 @@
             buf(3 * leaves, dtype=F32),
         ],
         compiler_params=params(),
-    )(ids, x_all, x_pts, w_all, coupling, near_blocks)
-    return pl.pallas_call(
+    )(coupling_pairs, near_pairs, coupling_count, x_all, x_pts, w_all, coupling, near_blocks)
+    out = pl.pallas_call(
         functools.partial(down_kernel, rows, cols),
-        out_shape=(jax.ShapeDtypeStruct((q, piece), BF),) * 2,
+        out_shape=jax.ShapeDtypeStruct((2 * q, piece), BF),
         in_specs=[VMEM] * 13,
-        out_specs=(VMEM,) * 2,
+        out_specs=VMEM,
         scratch_shapes=[
             buf(cols - 1, 2, packs),
             buf(deep, inner - 1, packs),
@@ -505,6 +510,7 @@
         y_part, z_part, n_part, n0, n2, order2, ubasis, vbasis, leaf_up_u, leaf_up_v,
         transfer_u, transfer_v, upper_coupling,
     )
+    return out[:q], out[q:]
 
 
 def solution(mesh):

time: 97 us -> 95.3 us (0.982); the launches traced: 96.3 us -> 96.5 us
  Pallas kernels: 90.2 us -> 93.5 us
  other arithmetic: 1.59 us -> 0 us
  local copies, waits for them, and re-layouts: 3.16 us -> 1.68 us
    pallas_call x1, Pallas kernels: 27.2 us -> 35.2 us  [per_device(): pl.pallas_call(slot_kernel, out_shape=(shape(cols, 2, packs), shape(rows,...]
    pallas_call x1, Pallas kernels: 33.8 us -> 29.1 us  [per_device(): pl.pallas_call(functools.partial(down_kernel, rows, cols), out_shape=jax....]
    unnamed x6 -> x0, local copies, waits for them, and re-layouts: 3.15 us -> none
    slice x0 -> x1, local copies, waits for them, and re-layouts: none -> 1.68 us  [per_device(): return (out[:q], out[q:])]
    slice x2 -> x0, other arithmetic: 1.53 us -> none  [the longest x1 0.77 us: per_device(): coupling_pairs[1] // leaves // cols * leaves + coupling_pairs[1] % leaves]
where the time goes in v3:
time: 95.3 us; the launch traced here: 96.5 us
  Pallas kernels  93.5 us (98%)
  local copies, waits for them, and re-layouts  1.68 us (2%)
  between operations  1.29 us (1%)
    pallas_call x1, Pallas kernels, per_device(): pl.pallas_call(slot_kernel, out_shape=(shape(cols, 2, packs), shape(rows,...  35.2 us
    pallas_call x1, Pallas kernels, per_device(): pl.pallas_call(functools.partial(up_kernel, rows, cols), out_shape=(shape...  29.2 us
    pallas_call x1, Pallas kernels, per_device(): pl.pallas_call(functools.partial(down_kernel, rows, cols), out_shape=jax....  29.1 us

profile of v3, /device:TPU:0, one launch (start us, length us, event | category | flops | bytes accessed | tf_op | source)
XLA Modules:
  0.0 96.5 jit_solution(10770484022300989621)
XLA Ops:
  1.3 29.2 %shard_map.158 = (bf16[8,8,64,128]{3,2,1,0:T(8,128)(2,1)}, bf16[3,8,64,128]{3,2,1,0:T(8,128)(2,1)}, bf16[4,2,8,64,128]{4,3,2,1,0:T(8,128)(2,1)}, bf16[4,64,128]{2,1,0:T(8,128)(2,1)}, bf16[8,64,128]{2,1,0:T(8,128)(2,1)}) custom-call(bf16[64,1024]{1,0:T(8,128)(2,1)} %x_ref.1, bf16[64,1024]{1,0:T(8,128)(2,1)} %w_ref.1, s32[1,1024]{1,0:T(1,128)} %bitcast.1, ...), custom_call_target="tpu_custom_call" | custom-call | tf_op jit(solution)/shard_map/pallas_call | solution.py:459
  30.5 35.2 %shard_map.159 = (bf16[4,2,8,64,128]{4,3,2,1,0:T(8,128)(2,1)}, bf16[8,8,64,128]{3,2,1,0:T(8,128)(2,1)}, bf16[3,8,64,128]{3,2,1,0:T(8,128)(2,1)}) custom-call(s32[2,512]{1,0:T(2,128)} %cp_ref.1, s32[2,256]{1,0:T(2,128)} %np_ref.1, s32[1]{0:T(128)S(6)} %copy.17.live_ref, bf16[8,8,64,128]{3,2,1,0:T(8,128)(2,1)} %get-tuple-element.10.x_ref, ...), custom_call_target="tpu_custom_call" | custom-call | tf_op jit(solution)/shard_map/pallas_call | solution.py:474
  65.7 29.1 %shard_map.160 = bf16[128,1024]{1,0:T(8,128)(2,1)} custom-call(bf16[4,2,8,64,128]{4,3,2,1,0:T(8,128)(2,1)} %get-tuple-element.13.y_ref, bf16[8,8,64,128]{3,2,1,0:T(8,128)(2,1)} %get-tuple-element.14.z_ref, bf16[3,8,64,128]{3,2,1,0:T(8,128)(2,1)} %get-tuple-element.15.n_ref, bf16[4,64,128]{2,1,0:T(8,128)(2,1)} %get-tuple-element.16.n0_ref, ...), custom_call_target="tpu_custom_call" | custom-call | tf_op jit(solution)/shard_map/pallas_call | solution.py:491
  94.8 1.7 %fusion = (bf16[64,1024]{1,0:T(8,128)(2,1)}, bf16[64,1024]{1,0:T(8,128)(2,1)}) fusion(bf16[128,1024]{1,0:T(8,128)(2,1)} %shard_map.160), kind=kLoop, calls=%fused_computation | loop fusion | bytes 524288 | tf_op jit(solution)/shard_map/slice | solution.py:513
